TPU v7x, 768 devices: a whole 4x8x12 slice. The times are simulated.
768 devices in a mesh: lat: 4 (over x_lo, core), lon: 12 (over z), ch: 16 (over y, x_hi).
Axes of the slice: x: 4 (x_hi: 2, x_lo: 2; x = x_hi * 2 + x_lo), y: 8, z: 12, core: 2. Of those that a mesh axis runs over, the one named last changes fastest.
Arguments:
- state_field: bfloat16 [256, 64, 3072], P('ch', 'lat', 'lon'), may hold values from -6 to 6
- land_mask: int32 [64, 3072], P('lat', 'lon'), may hold values 0 or 1
- partner: int32 [3072], replicated, may hold values from 0 to 3071, as said below
- kernel: bfloat16 [256, 49], P('ch'), may hold values from -0.875 to 0.875
- w_expand: bfloat16 [256, 1024], P(None, 'ch'), may hold values from -0.5 to 0.5
- w_project: bfloat16 [1024, 256], P('ch'), may hold values from -0.25 to 0.25
- cotangent: bfloat16 [256, 64, 3072], P('ch', 'lat', 'lon'), may hold values from -6 to 6
Outputs:
- state_out: bfloat16 [256, 64, 3072], P('ch', 'lat', 'lon')
- state_grad: bfloat16 [256, 64, 3072], P('ch', 'lat', 'lon')
Inputs may be any that keep to these rules, and one draw needn't show every extreme that they name: partner[i] = (s - i) mod 3072 for one s of the draw, so a column's partner's partner is the column itself.
All inputs are finite; a program needn't handle non-finite values. No bound on the sum of `land_mask` on one device may be relied on, other than what follows from the above.
Results may differ from a plain program's by a relative error of at most 0.017.
Values may be sent and summed in bfloat16 or wider, within the bound.
A program may use at most 64 MiB of HBM per device.

v0:
```python
import jax
import jax.numpy as jnp
from jax import lax
from jax.sharding import PartitionSpec as P

EPSILON = 1e-06


def with_halo(value, sides, width):
    for axis, dim in sides:
        count, length = (lax.axis_size(axis), value.shape[dim])
        up = [(i, (i + 1) % count) for i in range(count)]
        down = [(j, i) for i, j in up]
        last = lax.slice_in_dim(value, length - width, length, axis=dim)
        first = lax.slice_in_dim(value, 0, width, axis=dim)
        before = lax.ppermute(last, axis, up)
        after = lax.ppermute(first, axis, down)
        value = jnp.concatenate([before, value, after], axis=dim)
    return value


def conv_taps(padded, kernel, out_rows, out_cols):
    running = jnp.zeros((padded.shape[0], out_rows, out_cols), jnp.float32)
    weight_tensors = kernel.astype(jnp.float32)
    for offset in range(49):
        row_off = offset // 7
        col_off = offset % 7
        window = padded[:, row_off : row_off + out_rows, col_off : col_off + out_cols].astype(
            jnp.float32
        )
        running = running + weight_tensors[:, offset][:, None, None] * window
    return running


def gelu_parts(hidden):
    normal_cdf = 0.5 * (1.0 + lax.erf(hidden * 0.7071067811865476))
    return (
        hidden * normal_cdf,
        normal_cdf + hidden * jnp.exp(-0.5 * hidden * hidden) * 0.3989422804014327,
    )


def norm_stats(depth_half):
    values = depth_half.astype(jnp.float32)
    centre = jnp.mean(values, axis=0, keepdims=True)
    spread = values - centre
    inv_scale = lax.rsqrt(jnp.mean(spread * spread, axis=0, keepdims=True) + EPSILON)
    return (spread * inv_scale, inv_scale)


def norm_back(partial_value, normed, inv_scale, over_axis):
    mean_plain = jnp.mean(partial_value, axis=over_axis, keepdims=True)
    mean_cross = jnp.mean(partial_value * normed, axis=over_axis, keepdims=True)
    return inv_scale * (partial_value - mean_plain - normed * mean_cross)


def on_device(state_field, land_mask, partner, kernel, w_expand, w_project, cotangent):
    channels_here, row_count, col_count = state_field.shape
    full_width = partner.shape[0]
    cell_count = row_count * col_count
    lat_last = lax.axis_index("lat") == lax.axis_size("lat") - 1
    lat_first = lax.axis_index("lat") == 0
    lon_start = lax.axis_index("lon") * col_count
    ocean_mask = land_mask.astype(jnp.float32)
    masked = state_field * land_mask.astype(jnp.bfloat16)
    row_ids = jnp.arange(row_count + 6)
    row_keep = jnp.logical_not(lat_first & (row_ids < 3) | lat_last & (row_ids >= row_count + 3))
    top_flag = lat_last.astype(jnp.bfloat16)
    fold_columns = partner[
        jnp.mod(lon_start + jnp.arange(-3, col_count + 3, dtype=jnp.int32), full_width)
    ]

    def with_rims(values):
        padded = with_halo(values, (("lat", 1), ("lon", 2)), 3)
        return padded * row_keep[None, :, None].astype(values.dtype)

    def fold_band(values):
        gathered = lax.all_gather(values[:, row_count - 3 :, :], "lon", axis=2, tiled=True)
        return jnp.take(gathered[:, ::-1, :], fold_columns, axis=2) * top_flag

    padded = with_rims(masked)
    padded = jnp.concatenate(
        [padded[:, : row_count + 3], padded[:, row_count + 3 :] + fold_band(masked)], axis=1
    )
    depth_half = conv_taps(padded, kernel, row_count, col_count).astype(jnp.bfloat16)
    masked_cot = cotangent * land_mask.astype(jnp.bfloat16)
    depth_flat = depth_half.reshape(channels_here, cell_count)
    cot_flat = masked_cot.reshape(channels_here, cell_count)
    full_depth, full_cot = (
        lax.all_gather(depth_flat, "ch", axis=0, tiled=True),
        lax.all_gather(cot_flat, "ch", axis=0, tiled=True),
    )
    normed, inv_scale = norm_stats(full_depth)
    hidden = lax.dot_general(
        w_expand,
        normed.astype(jnp.bfloat16),
        (((0,), (0,)), ((), ())),
        preferred_element_type=jnp.float32,
    )
    active, slope_term = gelu_parts(hidden)
    output_piece = lax.dot_general(
        w_project,
        active.astype(jnp.bfloat16),
        (((0,), (0,)), ((), ())),
        preferred_element_type=jnp.float32,
    )
    back_hidden = (
        jnp.dot(w_project, full_cot, preferred_element_type=jnp.float32) * slope_term
    ).astype(jnp.bfloat16)
    partial_norm = jnp.dot(w_expand, back_hidden, preferred_element_type=jnp.float32)
    gradient_piece = norm_back(partial_norm, normed, inv_scale, 0)
    mixed_flat, grad_flat = (
        lax.psum_scatter(
            output_piece.astype(jnp.bfloat16), "ch", scatter_dimension=0, tiled=True
        ).astype(jnp.float32),
        lax.psum_scatter(
            gradient_piece.astype(jnp.bfloat16), "ch", scatter_dimension=0, tiled=True
        ).astype(jnp.float32),
    )
    mixed = mixed_flat.reshape(channels_here, row_count, col_count)
    state_out = (ocean_mask * (state_field.astype(jnp.float32) + mixed)).astype(jnp.bfloat16)
    grad_depth = grad_flat.reshape(channels_here, row_count, col_count).astype(jnp.bfloat16)
    flipped = kernel.reshape(channels_here, 7, 7)[:, ::-1, ::-1].reshape(channels_here, 49)
    grad_masked = conv_taps(with_rims(grad_depth), flipped, row_count, col_count)
    folded = jnp.concatenate(
        [jnp.zeros((channels_here, 6, col_count + 6), jnp.bfloat16), fold_band(grad_depth)], axis=1
    )
    top_part = conv_taps(folded, kernel, 3, col_count)
    grad_masked = jnp.concatenate(
        [grad_masked[:, : row_count - 3], grad_masked[:, row_count - 3 :] + top_part], axis=1
    )
    state_grad = (masked_cot.astype(jnp.float32) + ocean_mask * grad_masked).astype(jnp.bfloat16)
    return (state_out, state_grad)


def solution(mesh):
    placed = (
        P("ch", "lat", "lon"),
        P("lat", "lon"),
        P(),
        P("ch", None),
        P(None, "ch"),
        P("ch", None),
        P("ch", "lat", "lon"),
    )
    return jax.shard_map(
        on_device,
        mesh=mesh,
        in_specs=placed,
        out_specs=(P("ch", "lat", "lon"), P("ch", "lat", "lon")),
        check_vma=False,
    )
```

profile of v0, /device:TPU:7, one launch (start us, length us, event | category | flops | bytes accessed | tf_op | source)
XLA Modules:
  0.0 740.4 jit_solution(7531950154984484586)
XLA Ops:
  9.1 3.0 collective-permute-start
  14.1 3.4 gather_fusion
  21.8 30.0 %all_gather.12 = bf16[16,3,3072]{2,0,1:T(8,128)(2,1)} all-gather(bf16[16,3,256]{2,0,1:T(8,128)(2,1)S(1)} %copy.203), channel_id=1, replica_groups=mesh['lat'=4,'lon'=12,'ch'=16] {'lon'}, dimensions={2}, use_global_device_ids=true | all-gather | bytes 319488 | tf_op jit(solution)/shard_map/all_gather | solution.py:78
  54.6 4.6 collective-permute-start.3
  59.7 4.2 copy.204
  63.9 10.8 %rev.9 = bf16[16,3,3072]{0,1,2:T(4,128)(2,1)} reverse(bf16[16,3,3072]{0,1,2:T(4,128)(2,1)S(1)} %copy.204), dimensions={1} | reverse | bytes 589824 | tf_op jit(solution)/shard_map/rev | solution.py:79
  74.7 2.9 gather_fusion.1
  80.4 5.5 add_convert_fusion
  87.5 91.8 %all-gather.3.cloned.1.call-done = bf16[256,4096]{1,0:T(8,128)(2,1)} async-done(((bf16[16,4096]{1,0:T(8,128)(2,1)}), bf16[256,4096]{1,0:T(8,128)(2,1)}) %all-gather.3.cloned.1.call-update) | async-done | bytes 2097168 | tf_op jit(solution)/shard_map/all_gather | solution.py:90
  184.3 92.5 %all-gather.5.cloned.1.call-done = bf16[256,4096]{1,0:T(8,128)(2,1)} async-done(((bf16[16,4096]{1,0:T(8,128)(2,1)}), bf16[256,4096]{1,0:T(8,128)(2,1)}) %all-gather.5.cloned.1.call-update) | async-done | bytes 2097168 | tf_op jit(solution)/shard_map/all_gather | solution.py:91
  276.9 5.1 fusion.8
  281.9 2.4 reduce_sum.38
  284.4 4.6 fusion.11
  290.2 2.9 copy.215
  296.2 207.0 %reduce-scatter.5.cloned.1.call-done = bf16[16,4096]{1,0:T(8,128)(2,1)} async-done(((bf16[256,4096]{1,0:T(8,128)(2,1)}), bf16[16,4096]{1,0:T(8,128)(2,1)}) %reduce-scatter.5.cloned.1.call-update) | async-done | bytes 131088 | tf_op jit(solution)/shard_map/reduce_scatter | solution.py:116
  504.1 8.1 %collective-permute-start.4 = (bf16[16,3,256]{2,0,1:T(8,128)(2,1)S(1)}, bf16[16,3,256]{2,0,1:T(8,128)(2,1)S(1)}, u32[]{:S(2)}, u32[]{:S(2)}) collective-permute-start(bf16[16,3,256]{2,0,1:T(8,128)(2,1)S(1)} %get-tuple-element.63), channel_id=1, source_target_pairs={{0,192},{192,384},{384,576},{576,0},{1,193},{193,385},{385,577},{5... | collective-permute-start | bytes 73736 | tf_op jit(solution)/shard_map/ppermute | solution.py:16
  512.2 22.8 %all_gather.15 = bf16[16,3,3072]{2,0,1:T(8,128)(2,1)} all-gather(bf16[16,3,256]{2,0,1:T(8,128)(2,1)S(1)} %get-tuple-element.63), channel_id=1, replica_groups=mesh['lat'=4,'lon'=12,'ch'=16] {'lon'}, dimensions={2}, use_global_device_ids=true | all-gather | bytes 319488 | tf_op jit(solution)/shard_map/all_gather | solution.py:78
  535.1 4.2 copy.212
  539.3 10.8 %rev.11 = bf16[16,3,3072]{0,1,2:T(4,128)(2,1)} reverse(bf16[16,3,3072]{0,1,2:T(4,128)(2,1)S(1)} %copy.212), dimensions={1} | reverse | bytes 589824 | tf_op jit(solution)/shard_map/rev | solution.py:79
  550.1 2.9 gather_fusion.2
  553.2 6.5 collective-permute-start.5
  563.6 4.3 collective-permute-start.7
  568.6 156.4 %reduce-scatter.7.cloned.1.call-done = bf16[16,4096]{1,0:T(8,128)(2,1)} async-done(((bf16[256,4096]{1,0:T(8,128)(2,1)}), bf16[16,4096]{1,0:T(8,128)(2,1)}) %reduce-scatter.7.cloned.1.call-update) | async-done | bytes 131088 | tf_op jit(solution)/shard_map/reduce_scatter | solution.py:113
  727.0 5.0 multiply_add_fusion
  (185 shorter events, 33.6 us)
Async XLA Ops:
  7.2 269.7 %copy-start = (bf16[64,256]{1,0:T(8,128)(2,1)S(1)}, bf16[64,256]{1,0:T(8,128)(2,1)}, u32[]{:S(2)}) copy-start(bf16[64,256]{1,0:T(8,128)(2,1)} %param.14) | copy-start | bytes 98308
  7.2 172.2 %all-gather.3.cloned.1.call-start = ((), (), s32[]{:S(2)}) async-start(), calls=%async_computation.2 | async-start | bytes 2228224 | tf_op jit(solution)/shard_map/all_gather | solution.py:90
  9.1 42.8 %collective-permute-start = (bf16[16,3,256]{2,1,0:T(4,128)(2,1)S(1)}, bf16[16,3,256]{2,1,0:T(4,128)(2,1)S(1)}, u32[]{:S(2)}, u32[]{:S(2)}) collective-permute-start(bf16[16,3,256]{2,1,0:T(4,128)(2,1)S(1)} %get-tuple-element.65), channel_id=1, source_target_pairs={{0,192},{192,384},{384,576},{576,0},{1,193},{193,385},{385,577},{5... | collective-permute-start | bytes 73736 | tf_op jit(solution)/shard_map/ppermute | solution.py:16
  12.1 39.9 %collective-permute-start.1 = (bf16[16,3,256]{2,1,0:T(4,128)(2,1)S(1)}, bf16[16,3,256]{2,1,0:T(4,128)(2,1)S(1)}, u32[]{:S(2)}, u32[]{:S(2)}) collective-permute-start(bf16[16,3,256]{2,1,0:T(4,128)(2,1)S(1)} %get-tuple-element.64), channel_id=1, source_target_pairs={{192,0},{384,192},{576,384},{0,576},{193,1},{385,193},{577,385},{1... | collective-permute-start | bytes 73736 | tf_op jit(solution)/shard_map/ppermute | solution.py:17
  19.8 60.5 %copy-start.6 = (f32[16]{0:T(128)}, f32[16]{0:T(128)S(1)}, u32[]{:S(2)}) copy-start(f32[16]{0:T(128)S(1)} %get-tuple-element.15) | copy-start | bytes 196
  19.8 60.5 %copy-start.8 = (f32[16]{0:T(128)}, f32[16]{0:T(128)S(1)}, u32[]{:S(2)}) copy-start(f32[16]{0:T(128)S(1)} %get-tuple-element.16) | copy-start | bytes 196
  19.8 60.6 %copy-start.10 = (f32[16]{0:T(128)}, f32[16]{0:T(128)S(1)}, u32[]{:S(2)}) copy-start(f32[16]{0:T(128)S(1)} %get-tuple-element.17) | copy-start | bytes 196
  19.8 60.6 %copy-start.12 = (f32[16]{0:T(128)}, f32[16]{0:T(128)S(1)}, u32[]{:S(2)}) copy-start(f32[16]{0:T(128)S(1)} %get-tuple-element.18) | copy-start | bytes 196
  19.8 60.6 %copy-start.14 = (f32[16]{0:T(128)}, f32[16]{0:T(128)S(1)}, u32[]{:S(2)}) copy-start(f32[16]{0:T(128)S(1)} %get-tuple-element.19) | copy-start | bytes 196
  52.7 25.1 %collective-permute-start.2 = (bf16[16,22,3]{2,0,1:T(8,128)(2,1)}, bf16[16,22,3]{2,0,1:T(8,128)(2,1)}, u32[]{:S(2)}, u32[]{:S(2)}) collective-permute-start(bf16[16,22,3]{2,0,1:T(8,128)(2,1)} %get-tuple-element.60), channel_id=1, source_target_pairs={{0,16},{16,32},{32,48},{48,64},{64,80},{80,96},{96,112},{112,128},... | collective-permute-start | bytes 6344 | tf_op jit(solution)/shard_map/ppermute | solution.py:16
  54.6 23.2 %collective-permute-start.3 = (bf16[16,22,3]{2,0,1:T(8,128)(2,1)}, bf16[16,22,3]{2,0,1:T(8,128)(2,1)}, u32[]{:S(2)}, u32[]{:S(2)}) collective-permute-start(bf16[16,22,3]{2,0,1:T(8,128)(2,1)} %get-tuple-element.61), channel_id=1, source_target_pairs={{16,0},{32,16},{48,32},{64,48},{80,64},{96,80},{112,96},{128,112},... | collective-permute-start | bytes 6344 | tf_op jit(solution)/shard_map/ppermute | solution.py:17
  63.9 16.5 %copy-start.16 = (f32[16]{0:T(128)S(1)}, f32[16]{0:T(128)}, u32[]{:S(2)}) copy-start(f32[16]{0:T(128)} %get-tuple-element.20) | copy-start | bytes 196
  80.4 103.2 %copy-start.4 = (bf16[256,64]{0,1:T(8,128)(2,1)S(1)}, bf16[256,64]{0,1:T(8,128)(2,1)}, u32[]{:S(2)}) copy-start(bf16[256,64]{0,1:T(8,128)(2,1)} %param.13) | copy-start | bytes 98308
  86.7 190.2 %all-gather.5.cloned.1.call-start = ((), (), s32[]{:S(2)}) async-start(), calls=%async_computation.3 | async-start | bytes 2228224 | tf_op jit(solution)/shard_map/all_gather | solution.py:91
  87.5 415.7 %reduce-scatter.5.cloned.1.call-start = ((), (), s32[]{:S(2)}) async-start(), calls=%async_computation.4 | async-start | bytes 2228224 | tf_op jit(solution)/shard_map/reduce_scatter | solution.py:116
  289.2 435.8 %reduce-scatter.7.cloned.1.call-start = ((), (), s32[]{:S(2)}) async-start(), calls=%async_computation.5 | async-start | bytes 2228224 | tf_op jit(solution)/shard_map/reduce_scatter | solution.py:113
  504.1 55.6 %collective-permute-start.4 = (bf16[16,3,256]{2,0,1:T(8,128)(2,1)S(1)}, bf16[16,3,256]{2,0,1:T(8,128)(2,1)S(1)}, u32[]{:S(2)}, u32[]{:S(2)}) collective-permute-start(bf16[16,3,256]{2,0,1:T(8,128)(2,1)S(1)} %get-tuple-element.63), channel_id=1, source_target_pairs={{0,192},{192,384},{384,576},{576,0},{1,193},{193,385},{385,577},{5... | collective-permute-start | bytes 73736 | tf_op jit(solution)/shard_map/ppermute | solution.py:16
  539.3 20.5 %copy-start.3 = (bf16[16,4096]{1,0:T(8,128)(2,1)S(1)}, bf16[16,4096]{1,0:T(8,128)(2,1)}, u32[]{:S(2)}) copy-start(bf16[16,4096]{1,0:T(8,128)(2,1)} %reduce-scatter.5.cloned.1.call-done) | copy-start | bytes 393220
  553.2 8.1 %collective-permute-start.5 = (bf16[16,3,256]{2,0,1:T(8,128)(2,1)S(1)}, bf16[16,3,256]{2,0,1:T(8,128)(2,1)S(1)}, u32[]{:S(2)}, u32[]{:S(2)}) collective-permute-start(bf16[16,3,256]{2,0,1:T(8,128)(2,1)S(1)} %get-tuple-element.62), channel_id=1, source_target_pairs={{192,0},{384,192},{576,384},{0,576},{193,1},{385,193},{577,385},{1... | collective-permute-start | bytes 73736 | tf_op jit(solution)/shard_map/ppermute | solution.py:17
  561.4 164.7 %collective-permute-start.6 = (bf16[16,22,3]{2,0,1:T(8,128)(2,1)S(1)}, bf16[16,22,3]{2,0,1:T(8,128)(2,1)S(1)}, u32[]{:S(2)}, u32[]{:S(2)}) collective-permute-start(bf16[16,22,3]{2,0,1:T(8,128)(2,1)S(1)} %get-tuple-element.58), channel_id=1, source_target_pairs={{0,16},{16,32},{32,48},{48,64},{64,80},{80,96},{96,112},{112,128},... | collective-permute-start | bytes 6344 | tf_op jit(solution)/shard_map/ppermute | solution.py:16
  563.6 162.5 %collective-permute-start.7 = (bf16[16,22,3]{2,0,1:T(8,128)(2,1)S(1)}, bf16[16,22,3]{2,0,1:T(8,128)(2,1)S(1)}, u32[]{:S(2)}, u32[]{:S(2)}) collective-permute-start(bf16[16,22,3]{2,0,1:T(8,128)(2,1)S(1)} %get-tuple-element.59), channel_id=1, source_target_pairs={{16,0},{32,16},{48,32},{64,48},{80,64},{96,80},{112,96},{128,112},... | collective-permute-start | bytes 6344 | tf_op jit(solution)/shard_map/ppermute | solution.py:17
  725.1 7.0 copy-start.17
  725.1 7.0 copy-start.18
  725.1 7.0 copy-start.19
  (45 other events, 291.8 us)
Sparse Core Ops, SparseCore 0:
  86.8 92.4 all-gather.2
  183.7 93.1 all-gather.4
  289.1 214.0 reduce-scatter.4
  508.1 216.8 reduce-scatter.6
where the time goes:
time: 748 us; the launch traced here: 740 us
  waiting for transfers between devices  549 us (73%)
  blocking collectives  52.8 us (7%)
  local copies, waits for them, and re-layouts  52.2 us (7%)
  starting transfers between devices  32.9 us (4%)
  other arithmetic  31.6 us (4%)
  between operations  14.9 us (2%)
    reduce_scatter x1, waiting for transfers between devices, on_device(): lax.psum_scatter(gradient_piece.astype(jnp.bfloat16), 'ch', scatter_dimen...  207 us
    reduce_scatter x1, waiting for transfers between devices, on_device(): lax.psum_scatter(output_piece.astype(jnp.bfloat16), 'ch', scatter_dimensi...  156 us
    all_gather x1, waiting for transfers between devices, on_device(): lax.all_gather(cot_flat, 'ch', axis=0, tiled=True)  92.5 us
    all_gather x1, waiting for transfers between devices, on_device(): lax.all_gather(depth_flat, 'ch', axis=0, tiled=True)  91.8 us
    all_gather x2, blocking collectives, fold_band(): lax.all_gather(values[:, row_count - 3:, :], 'lon', axis=2, tiled=True)  52.8 us
    rev x2, local copies, waits for them, and re-layouts, fold_band(): return jnp.take(gathered[:, ::-1, :], fold_columns, axis=2) * top_flag  21.6 us
    ppermute x4, starting transfers between devices, with_halo(): after = lax.ppermute(first, axis, down)  17.3 us
    ppermute x4, starting transfers between devices, with_halo(): before = lax.ppermute(last, axis, up)  15.3 us
  transfers between devices with their start and end apart: 12, of which 5 were waited for; matrix products, arithmetic and copies ran while one was open for 8% of the time, Pallas kernels for 0%

commit v1 on v0

--- a/solution.py
+++ b/solution.py
@@ -84,42 +84,32 @@
     )
     depth_half = conv_taps(padded, kernel, row_count, col_count).astype(jnp.bfloat16)
     masked_cot = cotangent * land_mask.astype(jnp.bfloat16)
-    depth_flat = depth_half.reshape(channels_here, cell_count)
-    cot_flat = masked_cot.reshape(channels_here, cell_count)
-    full_depth, full_cot = (
-        lax.all_gather(depth_flat, "ch", axis=0, tiled=True),
-        lax.all_gather(cot_flat, "ch", axis=0, tiled=True),
-    )
+    expand_all = lax.all_gather(w_expand, "ch", axis=1, tiled=True)
+    project_all = lax.all_gather(w_project, "ch", axis=0, tiled=True)
+    full_depth = lax.all_to_all(depth_half, "ch", 1, 0, tiled=True).reshape(-1, col_count)
+    full_cot = lax.all_to_all(masked_cot, "ch", 1, 0, tiled=True).reshape(-1, col_count)
     normed, inv_scale = norm_stats(full_depth)
     hidden = lax.dot_general(
-        w_expand,
+        expand_all,
         normed.astype(jnp.bfloat16),
         (((0,), (0,)), ((), ())),
         preferred_element_type=jnp.float32,
     )
     active, slope_term = gelu_parts(hidden)
-    output_piece = lax.dot_general(
-        w_project,
+    mixed_rows = lax.dot_general(
+        project_all,
         active.astype(jnp.bfloat16),
         (((0,), (0,)), ((), ())),
         preferred_element_type=jnp.float32,
-    )
+    ).astype(jnp.bfloat16)
     back_hidden = (
-        jnp.dot(w_project, full_cot, preferred_element_type=jnp.float32) * slope_term
+        jnp.dot(project_all, full_cot, preferred_element_type=jnp.float32) * slope_term
     ).astype(jnp.bfloat16)
-    partial_norm = jnp.dot(w_expand, back_hidden, preferred_element_type=jnp.float32)
-    gradient_piece = norm_back(partial_norm, normed, inv_scale, 0)
-    mixed_flat, grad_flat = (
-        lax.psum_scatter(
-            output_piece.astype(jnp.bfloat16), "ch", scatter_dimension=0, tiled=True
-        ).astype(jnp.float32),
-        lax.psum_scatter(
-            gradient_piece.astype(jnp.bfloat16), "ch", scatter_dimension=0, tiled=True
-        ).astype(jnp.float32),
-    )
-    mixed = mixed_flat.reshape(channels_here, row_count, col_count)
+    full_norm = jnp.dot(expand_all, back_hidden, preferred_element_type=jnp.float32)
+    grad_rows = norm_back(full_norm, normed, inv_scale, 0).astype(jnp.bfloat16)
+    mixed = lax.all_to_all(mixed_rows[:, None, :], "ch", 0, 1, tiled=True).astype(jnp.float32)
+    grad_depth = lax.all_to_all(grad_rows[:, None, :], "ch", 0, 1, tiled=True)
     state_out = (ocean_mask * (state_field.astype(jnp.float32) + mixed)).astype(jnp.bfloat16)
-    grad_depth = grad_flat.reshape(channels_here, row_count, col_count).astype(jnp.bfloat16)
     flipped = kernel.reshape(channels_here, 7, 7)[:, ::-1, ::-1].reshape(channels_here, 49)
     grad_masked = conv_taps(with_rims(grad_depth), flipped, row_count, col_count)
     folded = jnp.concatenate(

time: 748 us -> 286 us (0.38)
  the two profiles are of different devices: /device:TPU:7 before, /device:TPU:6 now
where the time goes in v1:
time: 286 us; the launch traced here: 285 us
  blocking collectives  141 us (49%)
  starting transfers between devices  54.4 us (19%)
  local copies, waits for them, and re-layouts  48.8 us (17%)
  other arithmetic  21.9 us (8%)
  waiting for transfers between devices  14.8 us (5%)
    all_gather x2, blocking collectives, fold_band(): lax.all_gather(values[:, row_count - 3:, :], 'lon', axis=2, tiled=True)  58.8 us
    all_gather x1, blocking collectives, on_device(): expand_all = lax.all_gather(w_expand, 'ch', axis=1, tiled=True)  42.8 us
    all_gather x1, blocking collectives, on_device(): project_all = lax.all_gather(w_project, 'ch', axis=0, tiled=True)  39.5 us
    rev x2, local copies, waits for them, and re-layouts, fold_band(): return jnp.take(gathered[:, ::-1, :], fold_columns, axis=2) * top_flag  21.6 us
    ppermute x4, starting transfers between devices, with_halo(): after = lax.ppermute(first, axis, down)  12.7 us
    ppermute x4, starting transfers between devices, with_halo(): before = lax.ppermute(last, axis, up)  10.3 us
    all_to_all x1, starting transfers between devices, on_device(): lax.all_to_all(depth_half, 'ch', 1, 0, tiled=True).reshape(-1, col_count)  9.4 us
    all_to_all x1, starting transfers between devices, on_device(): lax.all_to_all(masked_cot, 'ch', 1, 0, tiled=True).reshape(-1, col_count)  9.15 us
  transfers between devices with their start and end apart: 12, of which 3 were waited for; matrix products, arithmetic and copies ran while one was open for 18% of the time, Pallas kernels for 0%

profile of v1, /device:TPU:6, one launch (start us, length us, event | category | flops | bytes accessed | tf_op | source)
XLA Modules:
  0.0 284.6 jit_solution(16418888801405577809)
XLA Ops:
  2.5 2.2 collective-permute-start.1
  6.9 2.2 gather_fusion
  14.1 35.7 %all_gather.12 = bf16[16,3,3072]{2,0,1:T(8,128)(2,1)} all-gather(bf16[16,3,256]{2,0,1:T(8,128)(2,1)S(1)} %copy.259), channel_id=1, replica_groups=mesh['lat'=4,'lon'=12,'ch'=16] {'lon'}, dimensions={2}, use_global_device_ids=true | all-gather | bytes 319488 | tf_op jit(solution)/shard_map/all_gather | solution.py:78
  49.8 42.8 %all_gather.13 = bf16[256,1024]{0,1:T(8,128)(2,1)} all-gather(bf16[256,64]{0,1:T(8,128)(2,1)S(1)} %copy-done.3), channel_id=1, replica_groups=mesh['lat'=4,'lon'=12,'ch'=16] {'ch'}, dimensions={1}, use_global_device_ids=true | all-gather | bytes 557056 | tf_op jit(solution)/shard_map/all_gather | solution.py:87
  95.9 5.1 %collective-permute-start.3 = (bf16[16,22,3]{2,0,1:T(8,128)(2,1)}, bf16[16,22,3]{2,0,1:T(8,128)(2,1)}, u32[]{:S(2)}, u32[]{:S(2)}) collective-permute-start(bf16[16,22,3]{2,0,1:T(8,128)(2,1)} %get-tuple-element.63), channel_id=1, source_target_pairs={{16,0},{32,16},{48,32},{64,48},{80,64},{96,80},{112,96},{128,112},... | collective-permute-start | bytes 6344 | tf_op jit(solution)/shard_map/ppermute | solution.py:17
  102.6 4.2 %copy.260 = bf16[16,3,3072]{0,1,2:T(4,128)(2,1)S(1)} copy(bf16[16,3,3072]{2,0,1:T(8,128)(2,1)} %all_gather.12) | data formatting | bytes 589824 | tf_op jit(solution)/shard_map/all_gather | solution.py:78
  106.9 10.8 %rev.9 = bf16[16,3,3072]{0,1,2:T(4,128)(2,1)} reverse(bf16[16,3,3072]{0,1,2:T(4,128)(2,1)S(1)} %copy.260), dimensions={1} | reverse | bytes 589824 | tf_op jit(solution)/shard_map/rev | solution.py:79
  117.7 2.9 %gather_fusion.1 = bf16[262,16,3]{1,2,0:T(4,128)(2,1)S(1)} fusion(bf16[16,3,3072]{0,1,2:T(4,128)(2,1)} %rev.9, s32[1024]{0:T(1024)S(1)} %pad_clamp_fusion), kind=kCustom, calls=%fused_computation.clone | custom fusion | bytes 51352 | tf_op jit(solution)/shard_map/jit(_take)/gather | solution.py:79
  123.5 5.6 %add_convert_fusion = bf16[16,16,256]{2,1,0:T(8,128)(2,1)S(1)} fusion(bf16[16,3,262]{2,1,0:T(4,128)(2,1)S(1)} %slice_add_fusion.1, bf16[16,19,262]{2,1,0:T(8,128)(2,1)S(1)} %bitcast.183, bf16[16,22,262]{2,1,0:T(8,128)(2,1)S(1)} %copy_multiply_fusion.1, f32[16]{0:T(128)S(1)} %get-tuple-element.12, f32[16]{0:T(128)S(1)} %copy-done.6, f32[16]{0:T(128)S(1)} %copy-done.8, ...), kind=kLoop, calls=%fused_computation.75 | loop fusion | flops 13762560 | bytes 3988672 | tf_op jit(solution)/shard_map/convert_element_type | solution.py:85
  129.8 9.4 %all-to-all-start = ((bf16[16,16,256]{2,0,1:T(8,128)(2,1)}), bf16[16,16,256]{2,0,1:T(8,128)(2,1)S(1)}, u32[]{:S(2)}, u32[]{:S(2)}) async-start(bf16[16,16,256]{2,0,1:T(8,128)(2,1)} %copy.262), calls=%async_computation | async-start | bytes 262144 | tf_op jit(solution)/shard_map/all_to_all | solution.py:89
  139.2 39.5 %all_gather.14 = bf16[1024,256]{1,0:T(8,128)(2,1)S(1)} all-gather(bf16[64,256]{1,0:T(8,128)(2,1)S(1)} %copy-done.4), channel_id=1, replica_groups=mesh['lat'=4,'lon'=12,'ch'=16] {'ch'}, dimensions={0}, use_global_device_ids=true | all-gather | bytes 557056 | tf_op jit(solution)/shard_map/all_gather | solution.py:88
  178.6 9.2 %all-to-all-start.2 = ((bf16[16,16,256]{2,0,1:T(8,128)(2,1)}), bf16[16,16,256]{2,0,1:T(8,128)(2,1)S(1)}, u32[]{:S(2)}, u32[]{:S(2)}) async-start(bf16[16,16,256]{2,0,1:T(8,128)(2,1)} %copy.267), calls=%async_computation.2 | async-start | bytes 262144 | tf_op jit(solution)/shard_map/all_to_all | solution.py:90
  188.3 7.9 %all-to-all-done.2 = bf16[16,16,256]{2,0,1:T(8,128)(2,1)S(1)} async-done(((bf16[16,16,256]{2,0,1:T(8,128)(2,1)}), bf16[16,16,256]{2,0,1:T(8,128)(2,1)S(1)}, u32[]{:S(2)}, u32[]{:S(2)}) %all-to-all-start.2) | async-done | bytes 131104 | tf_op jit(solution)/shard_map/all_to_all | solution.py:90
  199.1 6.1 %all-to-all-start.3 = ((bf16[16,2,2048]{2,1,0:T(2,128)(2,1)}), bf16[16,2,2048]{2,1,0:T(2,128)(2,1)S(1)}, u32[]{:S(2)}, u32[]{:S(2)}) async-start(bf16[16,2,2048]{2,1,0:T(2,128)(2,1)} %reshape.294), calls=%async_computation.3 | async-start | bytes 262144 | tf_op jit(solution)/shard_map/all_to_all | solution.py:111
  207.6 6.0 %all-to-all-done.3 = bf16[16,2,2048]{2,1,0:T(2,128)(2,1)S(1)} async-done(((bf16[16,2,2048]{2,1,0:T(2,128)(2,1)}), bf16[16,2,2048]{2,1,0:T(2,128)(2,1)S(1)}, u32[]{:S(2)}, u32[]{:S(2)}) %all-to-all-start.3) | async-done | bytes 131104 | tf_op jit(solution)/shard_map/all_to_all | solution.py:111
  213.6 6.8 %all-to-all-start.1 = ((bf16[16,2,2048]{2,1,0:T(2,128)(2,1)}), bf16[16,2,2048]{2,1,0:T(2,128)(2,1)}, u32[]{:S(2)}, u32[]{:S(2)}) async-start(bf16[16,2,2048]{2,1,0:T(2,128)(2,1)} %reshape.292), calls=%async_computation.1 | async-start | bytes 262144 | tf_op jit(solution)/shard_map/all_to_all | solution.py:110
  222.5 2.4 collective-permute-start.4
  225.0 23.1 %all_gather.15 = bf16[16,3,3072]{2,0,1:T(8,128)(2,1)} all-gather(bf16[16,3,256]{2,0,1:T(8,128)(2,1)S(1)} %get-tuple-element.64), channel_id=1, replica_groups=mesh['lat'=4,'lon'=12,'ch'=16] {'lon'}, dimensions={2}, use_global_device_ids=true | all-gather | bytes 319488 | tf_op jit(solution)/shard_map/all_gather | solution.py:78
  248.1 4.2 %copy.270 = bf16[16,3,3072]{0,1,2:T(4,128)(2,1)S(1)} copy(bf16[16,3,3072]{2,0,1:T(8,128)(2,1)} %all_gather.15) | data formatting | bytes 589824 | tf_op jit(solution)/shard_map/all_gather | solution.py:78
  252.3 10.8 %rev.11 = bf16[16,3,3072]{0,1,2:T(4,128)(2,1)} reverse(bf16[16,3,3072]{0,1,2:T(4,128)(2,1)S(1)} %copy.270), dimensions={1} | reverse | bytes 589824 | tf_op jit(solution)/shard_map/rev | solution.py:79
  263.3 2.9 %gather_fusion.2 = bf16[262,16,3]{1,2,0:T(4,128)(2,1)S(1)} fusion(bf16[16,3,3072]{0,1,2:T(4,128)(2,1)} %rev.11, s32[1024]{0:T(1024)S(1)} %pad_clamp_fusion), kind=kCustom, calls=%fused_computation.1.clone | custom fusion | bytes 51352 | tf_op jit(solution)/shard_map/jit(_take)/gather | solution.py:79
  266.5 3.8 %collective-permute-start.6 = (bf16[16,22,3]{2,0,1:T(8,128)(2,1)S(1)}, bf16[16,22,3]{2,0,1:T(8,128)(2,1)S(1)}, u32[]{:S(2)}, u32[]{:S(2)}) collective-permute-start(bf16[16,22,3]{2,0,1:T(8,128)(2,1)S(1)} %get-tuple-element.60), channel_id=1, source_target_pairs={{0,16},{16,32},{32,48},{48,64},{64,80},{80,96},{96,112},{112,128},... | collective-permute-start | bytes 6344 | tf_op jit(solution)/shard_map/ppermute | solution.py:16
  270.3 3.4 %collective-permute-start.7 = (bf16[16,22,3]{2,0,1:T(8,128)(2,1)S(1)}, bf16[16,22,3]{2,0,1:T(8,128)(2,1)S(1)}, u32[]{:S(2)}, u32[]{:S(2)}) collective-permute-start(bf16[16,22,3]{2,0,1:T(8,128)(2,1)S(1)} %get-tuple-element.61), channel_id=1, source_target_pairs={{16,0},{32,16},{48,32},{64,48},{80,64},{96,80},{112,96},{128,112},... | collective-permute-start | bytes 6344 | tf_op jit(solution)/shard_map/ppermute | solution.py:17
  278.1 4.6 %multiply_add_fusion = f32[16,16,256]{2,1,0:T(8,128)S(1)} fusion(bf16[16,22,262]{2,1,0:T(8,128)(2,1)S(1)} %copy_multiply_fusion, f32[16]{0:T(128)S(1)} %copy-done.77, f32[16]{0:T(128)} %get-tuple-element.70, f32[16]{0:T(128)} %get-tuple-element.71, f32[16]{0:T(128)} %get-tuple-element.72, f32[16]{0:T(128)} %get-tuple-element.73, f32[16]{0:T(128)} %get-tuple-element.74, ...), kind=kLoop, calls=%fused_computation.74 | loop fusion | flops 9568256 | bytes 6687808 | tf_op jit(solution)/shard_map/add | solution.py:31
  (232 shorter events, 30.9 us)
Async XLA Ops:
  2.5 90.7 %collective-permute-start.1 = (bf16[16,3,256]{2,1,0:T(4,128)(2,1)S(1)}, bf16[16,3,256]{2,1,0:T(4,128)(2,1)S(1)}, u32[]{:S(2)}, u32[]{:S(2)}) collective-permute-start(bf16[16,3,256]{2,1,0:T(4,128)(2,1)S(1)} %get-tuple-element.66), channel_id=1, source_target_pairs={{192,0},{384,192},{576,384},{0,576},{193,1},{385,193},{577,385},{1... | collective-permute-start | bytes 73736 | tf_op jit(solution)/shard_map/ppermute | solution.py:17
  4.7 88.5 %collective-permute-start = (bf16[16,3,256]{2,1,0:T(4,128)(2,1)S(1)}, bf16[16,3,256]{2,1,0:T(4,128)(2,1)S(1)}, u32[]{:S(2)}, u32[]{:S(2)}) collective-permute-start(bf16[16,3,256]{2,1,0:T(4,128)(2,1)S(1)} %get-tuple-element.67), channel_id=1, source_target_pairs={{0,192},{192,384},{384,576},{576,0},{1,193},{193,385},{385,577},{5... | collective-permute-start | bytes 73736 | tf_op jit(solution)/shard_map/ppermute | solution.py:16
  10.7 90.9 %copy-start.29 = (f32[16]{0:T(128)}, f32[16]{0:T(128)S(1)}, u32[]{:S(2)}) copy-start(f32[16]{0:T(128)S(1)} %get-tuple-element.50) | copy-start | bytes 196
  10.7 90.9 %copy-start.30 = (f32[16]{0:T(128)}, f32[16]{0:T(128)S(1)}, u32[]{:S(2)}) copy-start(f32[16]{0:T(128)S(1)} %get-tuple-element.51) | copy-start | bytes 196
  10.7 90.9 %copy-start.31 = (f32[16]{0:T(128)}, f32[16]{0:T(128)S(1)}, u32[]{:S(2)}) copy-start(f32[16]{0:T(128)S(1)} %get-tuple-element.52) | copy-start | bytes 196
  10.8 90.9 %copy-start.32 = (f32[16]{0:T(128)}, f32[16]{0:T(128)S(1)}, u32[]{:S(2)}) copy-start(f32[16]{0:T(128)S(1)} %get-tuple-element.53) | copy-start | bytes 196
  10.8 90.9 %copy-start.33 = (f32[16]{0:T(128)}, f32[16]{0:T(128)S(1)}, u32[]{:S(2)}) copy-start(f32[16]{0:T(128)S(1)} %get-tuple-element.54) | copy-start | bytes 196
  10.8 90.9 %copy-start.34 = (f32[16]{0:T(128)}, f32[16]{0:T(128)S(1)}, u32[]{:S(2)}) copy-start(f32[16]{0:T(128)S(1)} %get-tuple-element.55) | copy-start | bytes 196
  10.8 90.9 %copy-start.35 = (f32[16]{0:T(128)}, f32[16]{0:T(128)S(1)}, u32[]{:S(2)}) copy-start(f32[16]{0:T(128)S(1)} %get-tuple-element.56) | copy-start | bytes 196
  10.8 90.9 %copy-start.36 = (f32[16]{0:T(128)}, f32[16]{0:T(128)S(1)}, u32[]{:S(2)}) copy-start(f32[16]{0:T(128)S(1)} %get-tuple-element.57) | copy-start | bytes 196
  10.8 90.9 %copy-start.37 = (f32[16]{0:T(128)}, f32[16]{0:T(128)S(1)}, u32[]{:S(2)}) copy-start(f32[16]{0:T(128)S(1)} %get-tuple-element.58) | copy-start | bytes 196
  10.8 90.9 %copy-start.38 = (f32[16]{0:T(128)}, f32[16]{0:T(128)S(1)}, u32[]{:S(2)}) copy-start(f32[16]{0:T(128)S(1)} %get-tuple-element.59) | copy-start | bytes 196
  11.4 90.4 %copy-start.40 = (f32[16]{0:T(128)}, f32[16]{0:T(128)S(1)}, u32[]{:S(2)}) copy-start(f32[16]{0:T(128)S(1)} %get-tuple-element.34) | copy-start | bytes 196
  11.4 90.4 %copy-start.41 = (f32[16]{0:T(128)}, f32[16]{0:T(128)S(1)}, u32[]{:S(2)}) copy-start(f32[16]{0:T(128)S(1)} %get-tuple-element.35) | copy-start | bytes 196
  94.0 26.8 %collective-permute-start.2 = (bf16[16,22,3]{2,0,1:T(8,128)(2,1)}, bf16[16,22,3]{2,0,1:T(8,128)(2,1)}, u32[]{:S(2)}, u32[]{:S(2)}) collective-permute-start(bf16[16,22,3]{2,0,1:T(8,128)(2,1)} %get-tuple-element.62), channel_id=1, source_target_pairs={{0,16},{16,32},{32,48},{48,64},{64,80},{80,96},{96,112},{112,128},... | collective-permute-start | bytes 6344 | tf_op jit(solution)/shard_map/ppermute | solution.py:16
  95.9 24.9 %collective-permute-start.3 = (bf16[16,22,3]{2,0,1:T(8,128)(2,1)}, bf16[16,22,3]{2,0,1:T(8,128)(2,1)}, u32[]{:S(2)}, u32[]{:S(2)}) collective-permute-start(bf16[16,22,3]{2,0,1:T(8,128)(2,1)} %get-tuple-element.63), channel_id=1, source_target_pairs={{16,0},{32,16},{48,32},{64,48},{80,64},{96,80},{112,96},{128,112},... | collective-permute-start | bytes 6344 | tf_op jit(solution)/shard_map/ppermute | solution.py:17
  129.8 48.9 %all-to-all-start = ((bf16[16,16,256]{2,0,1:T(8,128)(2,1)}), bf16[16,16,256]{2,0,1:T(8,128)(2,1)S(1)}, u32[]{:S(2)}, u32[]{:S(2)}) async-start(bf16[16,16,256]{2,0,1:T(8,128)(2,1)} %copy.262), calls=%async_computation | async-start | bytes 262144 | tf_op jit(solution)/shard_map/all_to_all | solution.py:89
  178.6 17.6 %all-to-all-start.2 = ((bf16[16,16,256]{2,0,1:T(8,128)(2,1)}), bf16[16,16,256]{2,0,1:T(8,128)(2,1)S(1)}, u32[]{:S(2)}, u32[]{:S(2)}) async-start(bf16[16,16,256]{2,0,1:T(8,128)(2,1)} %copy.267), calls=%async_computation.2 | async-start | bytes 262144 | tf_op jit(solution)/shard_map/all_to_all | solution.py:90
  199.1 14.6 %all-to-all-start.3 = ((bf16[16,2,2048]{2,1,0:T(2,128)(2,1)}), bf16[16,2,2048]{2,1,0:T(2,128)(2,1)S(1)}, u32[]{:S(2)}, u32[]{:S(2)}) async-start(bf16[16,2,2048]{2,1,0:T(2,128)(2,1)} %reshape.294), calls=%async_computation.3 | async-start | bytes 262144 | tf_op jit(solution)/shard_map/all_to_all | solution.py:111
  213.6 60.8 %all-to-all-start.1 = ((bf16[16,2,2048]{2,1,0:T(2,128)(2,1)}), bf16[16,2,2048]{2,1,0:T(2,128)(2,1)}, u32[]{:S(2)}, u32[]{:S(2)}) async-start(bf16[16,2,2048]{2,1,0:T(2,128)(2,1)} %reshape.292), calls=%async_computation.1 | async-start | bytes 262144 | tf_op jit(solution)/shard_map/all_to_all | solution.py:110
  220.6 45.8 %collective-permute-start.5 = (bf16[16,3,256]{2,0,1:T(8,128)(2,1)S(1)}, bf16[16,3,256]{2,0,1:T(8,128)(2,1)S(1)}, u32[]{:S(2)}, u32[]{:S(2)}) collective-permute-start(bf16[16,3,256]{2,0,1:T(8,128)(2,1)S(1)} %get-tuple-element.65), channel_id=1, source_target_pairs={{192,0},{384,192},{576,384},{0,576},{193,1},{385,193},{577,385},{1... | collective-permute-start | bytes 73736 | tf_op jit(solution)/shard_map/ppermute | solution.py:17
  222.5 43.9 %collective-permute-start.4 = (bf16[16,3,256]{2,0,1:T(8,128)(2,1)S(1)}, bf16[16,3,256]{2,0,1:T(8,128)(2,1)S(1)}, u32[]{:S(2)}, u32[]{:S(2)}) collective-permute-start(bf16[16,3,256]{2,0,1:T(8,128)(2,1)S(1)} %get-tuple-element.64), channel_id=1, source_target_pairs={{0,192},{192,384},{384,576},{576,0},{1,193},{193,385},{385,577},{5... | collective-permute-start | bytes 73736 | tf_op jit(solution)/shard_map/ppermute | solution.py:16
  266.5 9.3 %collective-permute-start.6 = (bf16[16,22,3]{2,0,1:T(8,128)(2,1)S(1)}, bf16[16,22,3]{2,0,1:T(8,128)(2,1)S(1)}, u32[]{:S(2)}, u32[]{:S(2)}) collective-permute-start(bf16[16,22,3]{2,0,1:T(8,128)(2,1)S(1)} %get-tuple-element.60), channel_id=1, source_target_pairs={{0,16},{16,32},{32,48},{48,64},{64,80},{80,96},{96,112},{112,128},... | collective-permute-start | bytes 6344 | tf_op jit(solution)/shard_map/ppermute | solution.py:16
  270.3 6.4 %collective-permute-start.7 = (bf16[16,22,3]{2,0,1:T(8,128)(2,1)S(1)}, bf16[16,22,3]{2,0,1:T(8,128)(2,1)S(1)}, u32[]{:S(2)}, u32[]{:S(2)}) collective-permute-start(bf16[16,22,3]{2,0,1:T(8,128)(2,1)S(1)} %get-tuple-element.61), channel_id=1, source_target_pairs={{16,0},{32,16},{48,32},{64,48},{80,64},{96,80},{112,96},{128,112},... | collective-permute-start | bytes 6344 | tf_op jit(solution)/shard_map/ppermute | solution.py:17
  (66 other events, 2071.5 us)

commit v2 on v1

v2 whole, which is shorter than its diff:
```python
import functools

import jax
import jax.numpy as jnp
from jax import lax
from jax.experimental import pallas as pl
from jax.experimental.pallas import tpu as pltpu
from jax.sharding import PartitionSpec as P

EPSILON = 1e-06
HALO = 3
EDGE = 128
TAPS = 7
DIRECTIONS = ((-1, 0), (1, 0), (0, -1), (0, 1), (-1, -1), (-1, 1), (1, -1), (1, 1))
MESH = pl.DeviceIdType.MESH
F32 = jnp.float32
BF16 = jnp.bfloat16


def dot(a, b, dims=((1,), (0,))):
    return lax.dot_general(a, b, (dims, ((), ())), preferred_element_type=F32)


def gelu_parts(hidden):
    normal_cdf = 0.5 * (1.0 + lax.erf(hidden * 0.7071067811865476))
    return (
        hidden * normal_cdf,
        normal_cdf + hidden * jnp.exp(-0.5 * hidden * hidden) * 0.3989422804014327,
    )


def block_kernel(
    sizes,
    partner_ref,
    state_ref,
    mask_ref,
    kernel_ref,
    expand_ref,
    project_ref,
    cot_ref,
    out_ref,
    grad_ref,
    ext,
    ext_back,
    fold_rows,
    fold_rows_back,
    pick,
    taps,
    acc,
    cot_rows,
    cot_all,
    depth_rows,
    depth_all,
    weights,
    normed_ref,
    mixed_send,
    grad_send,
    mixed_rows,
    halo_send,
    halo_recv,
    halo_send_back,
    halo_recv_back,
    send,
    recv,
):
    n_lat, n_lon, n_ch, rows, chans, cols, hidden_here = sizes
    wide = cols + 2 * EDGE
    cells = rows * chans
    lat, lon, me = lax.axis_index("lat"), lax.axis_index("lon"), lax.axis_index("ch")
    lat_last = lat == n_lat - 1
    part = lax.rem(lat, 2)
    sibling = lat + 1 - 2 * part
    own_rows = pl.ds(HALO, rows)
    own_lanes = pl.ds(EDGE, cols)

    def exists(dl):
        return jnp.logical_and(lat + dl >= 0, lat + dl < n_lat)

    def at(dl, do):
        return {"lat": lat + dl, "lon": lax.rem(lon + do + n_lon, n_lon), "ch": me}

    barrier = pltpu.get_barrier_semaphore()

    def greet_channel(i, carry):
        pl.semaphore_signal(
            barrier,
            device_id={"lat": lat, "lon": lon, "ch": lax.rem(me + i, n_ch)},
            device_id_type=MESH,
        )
        return carry

    def greet_fold(i, carry):
        pl.semaphore_signal(
            barrier,
            device_id={"lat": lat, "lon": lax.rem(lon + i, n_lon), "ch": me},
            device_id_type=MESH,
        )
        return carry

    for dl, do in DIRECTIONS:

        @pl.when(exists(dl))
        def _():
            pl.semaphore_signal(barrier, device_id=at(dl, do), device_id_type=MESH)

    lax.fori_loop(1, n_ch, greet_channel, 0)

    @pl.when(lat_last)
    def _():
        lax.fori_loop(1, n_lon, greet_fold, 0)

    swap_row = lax.broadcasted_iota(jnp.int32, (cells, cells), 0)
    swap_col = lax.broadcasted_iota(jnp.int32, (cells, cells), 1)
    to_rows = (swap_col == lax.rem(swap_row, chans) * rows + swap_row // chans).astype(BF16)
    mask_half = mask_ref[...].astype(BF16)
    masked = (state_ref[...] * mask_half[None]).reshape(cells, cols)
    ext[own_rows, :, own_lanes] = (
        dot(to_rows, masked).astype(BF16).reshape(rows, chans, cols)
    )
    masked_cot = (cot_ref[...] * mask_half[None]).reshape(cells, cols)
    cot_rows[...] = dot(to_rows, masked_cot).astype(BF16).reshape(rows, chans, cols)
    cot_all[me] = cot_rows[me]

    @pl.when(part == 0)
    def _():
        unit_row = lax.broadcasted_iota(jnp.int32, (n_ch * chans, n_ch * chans), 0)
        unit_col = lax.broadcasted_iota(jnp.int32, (n_ch * chans, n_ch * chans), 1)
        unit = (unit_row == unit_col).astype(BF16)
        weights[0, me] = dot(expand_ref[...], unit, ((0,), (0,))).astype(BF16)

    @pl.when(part == 1)
    def _():
        weights[1, me] = project_ref[...]

    for t in range(TAPS * TAPS):
        tap = jnp.broadcast_to(kernel_ref[:, t : t + 1].astype(F32), (chans, EDGE))
        taps[0, t] = tap
        taps[1, TAPS * TAPS - 1 - t] = tap

    @pl.when(lat == 0)
    def _():
        ext[0:HALO] = jnp.zeros((HALO, chans, wide), BF16)
        ext_back[0:HALO] = jnp.zeros((HALO, chans, wide), BF16)

    @pl.when(lat_last)
    def _():
        fold_rows[lon] = ext[pl.ds(rows, HALO), :, own_lanes]

    neighbours = sum(
        (exists(dl).astype(jnp.int32) for dl, _ in DIRECTIONS), jnp.int32(n_ch - 1)
    ) + jnp.where(lat_last, n_lon - 1, 0)
    pl.semaphore_wait(barrier, neighbours)

    def halo_copy(buffer, d, send_sems, recv_sems):
        dl, do = DIRECTIONS[d]
        src_rows, dst_rows = {
            -1: (pl.ds(HALO, HALO), pl.ds(HALO + rows, HALO)),
            0: (own_rows, own_rows),
            1: (pl.ds(rows, HALO), pl.ds(0, HALO)),
        }[dl]
        src_lanes, dst_lanes = {
            -1: (pl.ds(EDGE, EDGE), pl.ds(EDGE + cols, EDGE)),
            0: (own_lanes, own_lanes),
            1: (pl.ds(cols, EDGE), pl.ds(0, EDGE)),
        }[do]
        return pltpu.make_async_remote_copy(
            src_ref=buffer.at[src_rows, :, src_lanes],
            dst_ref=buffer.at[dst_rows, :, dst_lanes],
            send_sem=send_sems.at[d],
            recv_sem=recv_sems.at[d],
            device_id=at(dl, do),
            device_id_type=MESH,
        )

    def halo_start(buffer, send_sems, recv_sems):
        for d, (dl, _) in enumerate(DIRECTIONS):
            pl.when(exists(dl))(lambda d=d: halo_copy(buffer, d, send_sems, recv_sems).start())

    def halo_arrived(buffer, send_sems, recv_sems):
        for d, (dl, _) in enumerate(DIRECTIONS):
            pl.when(exists(-dl))(
                lambda d=d: halo_copy(buffer, d, send_sems, recv_sems).wait_recv()
            )

    def halo_sent(buffer, send_sems, recv_sems):
        for d, (dl, _) in enumerate(DIRECTIONS):
            pl.when(exists(dl))(
                lambda d=d: halo_copy(buffer, d, send_sems, recv_sems).wait_send()
            )

    def fold_copy(buffer, gathered, i, k):
        return pltpu.make_async_remote_copy(
            src_ref=buffer.at[pl.ds(rows, HALO), :, own_lanes],
            dst_ref=gathered.at[lon],
            send_sem=send.at[k],
            recv_sem=recv.at[k],
            device_id={"lat": lat, "lon": lax.rem(lon + i, n_lon), "ch": me},
            device_id_type=MESH,
        )

    def several(gathered, count, k):
        whole = gathered.at[pl.ds(0, count)]
        return pltpu.make_async_remote_copy(
            src_ref=whole,
            dst_ref=whole,
            send_sem=send.at[k],
            recv_sem=recv.at[k],
            device_id={"lat": lat, "lon": lon, "ch": lax.rem(me + 1, n_ch)},
            device_id_type=MESH,
        )

    def channel_copies(make_src, make_dst, k):
        def step(i, carry):
            peer = lax.rem(me + i, n_ch)
            pltpu.make_async_remote_copy(
                src_ref=make_src(peer),
                dst_ref=make_dst(),
                send_sem=send.at[k],
                recv_sem=recv.at[k],
                device_id={"lat": lat, "lon": lon, "ch": peer},
                device_id_type=MESH,
            ).start()
            return carry

        lax.fori_loop(1, n_ch, step, 0)

    def fold_start(buffer, gathered, k):
        def step(i, carry):
            fold_copy(buffer, gathered, i, k).start()
            return carry

        lax.fori_loop(1, n_lon, step, 0)

    halo_start(ext, halo_send, halo_recv)

    @pl.when(lat_last)
    def _():
        fold_start(ext, fold_rows, 0)

    own_weights = weights.at[part, me]
    channel_copies(lambda peer: own_weights, lambda: own_weights, 1)
    channel_copies(lambda peer: cot_rows.at[peer], lambda: cot_all.at[me], 2)

    full_width = n_lon * cols
    turn = partner_ref[0]
    first = lax.rem(turn - lon * cols - (cols + HALO - 1) + 2 * full_width, full_width)
    first_block = first // cols
    origin = lax.rem(turn - lon * cols + EDGE - first_block * cols + 3 * full_width, full_width)

    @pl.when(lat_last)
    def _():
        source = lax.broadcasted_iota(jnp.int32, (3 * cols, wide), 0)
        want = origin - lax.broadcasted_iota(jnp.int32, (3 * cols, wide), 1)
        want = jnp.where(want < 0, want + full_width, want)
        pick[...] = (source == want).astype(BF16)

    def fold_fill(buffer, gathered):
        found = jnp.zeros((HALO * chans, wide), F32)
        for j in range(3):
            piece = gathered[lax.rem(first_block + j, n_lon)].reshape(HALO * chans, cols)
            found = found + dot(piece, pick[j * cols : (j + 1) * cols, :])
        found = found.astype(BF16).reshape(HALO, chans, wide)
        for j in range(HALO):
            buffer[HALO + rows + j] = found[HALO - 1 - j]

    def conv(buffer, table_of):
        acc[...] = jnp.zeros(acc.shape, F32)

        def step(e, carry):
            table = table_of(e)
            line = buffer[e].astype(F32)
            shifted = [
                line[:, EDGE - HALO + b : EDGE - HALO + b + cols] for b in range(TAPS)
            ]
            for a in range(TAPS):
                total = acc[e - a + TAPS - 1]
                for b in range(TAPS):
                    tap = taps[table, a * TAPS + b]
                    total = total + jnp.concatenate([tap] * (cols // EDGE), axis=1) * shifted[b]
                acc[e - a + TAPS - 1] = total
            return carry

        lax.fori_loop(0, rows + 2 * HALO, step, 0)

    halo_arrived(ext, halo_send, halo_recv)

    @pl.when(lat_last)
    def _():
        several(fold_rows, n_lon - 1, 0).wait_recv()
        fold_fill(ext, fold_rows)

    conv(ext, lambda e: 0)
    depth_rows[...] = acc[pl.ds(TAPS - 1, rows)].astype(BF16)
    channel_copies(lambda peer: depth_rows.at[peer], lambda: depth_all.at[me], 3)
    depth_all[me] = depth_rows[me]

    def swap_weights():
        return pltpu.make_async_remote_copy(
            src_ref=weights.at[part],
            dst_ref=weights.at[part],
            send_sem=send.at[4],
            recv_sem=recv.at[4],
            device_id={"lat": sibling, "lon": lon, "ch": me},
            device_id_type=MESH,
        )

    several(weights.at[part], n_ch - 1, 1).wait_recv()
    swap_weights().start()
    several(cot_all, n_ch - 1, 2).wait_recv()
    several(depth_all, n_ch - 1, 3).wait_recv()

    channels = n_ch * chans
    values = depth_all[...].reshape(channels, cols).astype(F32)
    spread = values - jnp.mean(values, axis=0, keepdims=True)
    inv_scale = lax.rsqrt(jnp.mean(spread * spread, axis=0, keepdims=True) + EPSILON)
    normed_ref[...] = spread * inv_scale
    normed_half = normed_ref[...].astype(BF16)
    cot_here = cot_all[...].reshape(channels, cols)
    pltpu.make_async_remote_copy(
        src_ref=weights.at[1 - part],
        dst_ref=weights.at[1 - part],
        send_sem=send.at[4],
        recv_sem=recv.at[4],
        device_id={"lat": sibling, "lon": lon, "ch": me},
        device_id_type=MESH,
    ).wait_recv()

    mixed = jnp.zeros((channels, cols), F32)
    back_norm = jnp.zeros((channels, cols), F32)
    per_chunk = n_ch // 4
    for j in range(4):
        span = slice(j * per_chunk, (j + 1) * per_chunk)
        expand = weights[0, span].reshape(per_chunk * hidden_here, channels)
        project = weights[1, span].reshape(per_chunk * hidden_here, channels)
        active, slope = gelu_parts(dot(expand, normed_half))
        back_hidden = (dot(project, cot_here) * slope).astype(BF16)
        mixed = mixed + dot(project, active.astype(BF16), ((0,), (0,)))
        back_norm = back_norm + dot(expand, back_hidden, ((0,), (0,)))
    normed = normed_ref[...]
    mean_plain = jnp.mean(back_norm, axis=0, keepdims=True)
    mean_cross = jnp.mean(back_norm * normed, axis=0, keepdims=True)
    grad_send[...] = (
        (inv_scale * (back_norm - mean_plain - normed * mean_cross))
        .astype(BF16)
        .reshape(n_ch, chans, cols)
    )
    back_row = ext_back.at[HALO + me, :, own_lanes]
    channel_copies(lambda peer: grad_send.at[peer], lambda: back_row, 5)
    ext_back[HALO + me, :, own_lanes] = grad_send[me]
    mixed_send[...] = mixed.astype(BF16).reshape(n_ch, chans, cols)
    channel_copies(lambda peer: mixed_send.at[peer], lambda: mixed_rows.at[me], 6)
    mixed_rows[me] = mixed_send[me]

    several(grad_send, n_ch - 1, 5).wait_recv()
    halo_start(ext_back, halo_send_back, halo_recv_back)

    @pl.when(lat_last)
    def _():
        fold_start(ext_back, fold_rows_back, 7)
        fold_rows_back[lon] = ext_back[pl.ds(rows, HALO), :, own_lanes]

    several(mixed_rows, n_ch - 1, 6).wait_recv()
    to_chans = (swap_col == lax.rem(swap_row, rows) * chans + swap_row // rows).astype(BF16)
    mixed_here = dot(to_chans, mixed_rows[...].reshape(cells, cols)).reshape(chans, rows, cols)
    ocean = mask_ref[...].astype(F32)
    out_ref[...] = (ocean[None] * (state_ref[...].astype(F32) + mixed_here)).astype(BF16)

    halo_arrived(ext_back, halo_send_back, halo_recv_back)

    @pl.when(lat_last)
    def _():
        several(fold_rows_back, n_lon - 1, 7).wait_recv()
        fold_fill(ext_back, fold_rows_back)

    fold_from = jnp.where(lat_last, HALO + rows, rows + 2 * HALO)
    conv(ext_back, lambda e: jnp.where(e >= fold_from, 0, 1))
    grad_rows = (
        cot_rows[...].astype(F32) + ocean[:, None, :] * acc[pl.ds(TAPS - 1, rows)]
    ).astype(BF16)
    grad_ref[...] = (
        dot(to_chans, grad_rows.reshape(cells, cols)).astype(BF16).reshape(chans, rows, cols)
    )

    halo_sent(ext, halo_send, halo_recv)
    halo_sent(ext_back, halo_send_back, halo_recv_back)

    @pl.when(lat_last)
    def _():
        several(fold_rows, n_lon - 1, 0).wait_send()
        several(fold_rows_back, n_lon - 1, 7).wait_send()

    several(weights.at[part], n_ch - 1, 1).wait_send()
    several(cot_rows, n_ch - 1, 2).wait_send()
    several(depth_rows, n_ch - 1, 3).wait_send()
    swap_weights().wait_send()
    several(grad_send, n_ch - 1, 5).wait_send()
    several(mixed_send, n_ch - 1, 6).wait_send()


def on_device(state_field, land_mask, partner, kernel, w_expand, w_project, cotangent):
    n_lat, n_lon, n_ch = (lax.axis_size(name) for name in ("lat", "lon", "ch"))
    chans, rows, cols = state_field.shape
    hidden_here = w_project.shape[0]
    assert rows == n_ch and n_lat % 2 == 0
    wide = cols + 2 * EDGE
    channels = n_ch * chans
    sizes = (n_lat, n_lon, n_ch, rows, chans, cols, hidden_here)
    vmem = pl.BlockSpec(memory_space=pltpu.VMEM)
    tile_rows = rows + 2 * HALO
    return pl.pallas_call(
        functools.partial(block_kernel, sizes),
        out_shape=(jax.ShapeDtypeStruct(state_field.shape, BF16),) * 2,
        in_specs=[pl.BlockSpec(memory_space=pltpu.SMEM)] + [vmem] * 6,
        out_specs=(vmem, vmem),
        scratch_shapes=[
            pltpu.VMEM((tile_rows, chans, wide), BF16),
            pltpu.VMEM((tile_rows, chans, wide), BF16),
            pltpu.VMEM((n_lon, HALO, chans, cols), BF16),
            pltpu.VMEM((n_lon, HALO, chans, cols), BF16),
            pltpu.VMEM((3 * cols, wide), BF16),
            pltpu.VMEM((2, TAPS * TAPS, chans, EDGE), F32),
            pltpu.VMEM((rows + 2 * (TAPS - 1), chans, cols), F32),
            pltpu.VMEM((rows, chans, cols), BF16),
            pltpu.VMEM((n_ch, chans, cols), BF16),
            pltpu.VMEM((rows, chans, cols), BF16),
            pltpu.VMEM((n_ch, chans, cols), BF16),
            pltpu.VMEM((2, n_ch, hidden_here, channels), BF16),
            pltpu.VMEM((channels, cols), F32),
            pltpu.VMEM((n_ch, chans, cols), BF16),
            pltpu.VMEM((n_ch, chans, cols), BF16),
            pltpu.VMEM((n_ch, chans, cols), BF16),
            pltpu.SemaphoreType.DMA((8,)),
            pltpu.SemaphoreType.DMA((8,)),
            pltpu.SemaphoreType.DMA((8,)),
            pltpu.SemaphoreType.DMA((8,)),
            pltpu.SemaphoreType.DMA((8,)),
            pltpu.SemaphoreType.DMA((8,)),
        ],
        compiler_params=pltpu.CompilerParams(
            collective_id=0, has_side_effects=True, vmem_limit_bytes=48 * 1024 * 1024
        ),
        name="ocean_block",
    )(partner, state_field, land_mask, kernel, w_expand, w_project, cotangent)


def solution(mesh):
    placed = (
        P("ch", "lat", "lon"),
        P("lat", "lon"),
        P(),
        P("ch", None),
        P(None, "ch"),
        P("ch", None),
        P("ch", "lat", "lon"),
    )
    return jax.shard_map(
        on_device,
        mesh=mesh,
        in_specs=placed,
        out_specs=(P("ch", "lat", "lon"), P("ch", "lat", "lon")),
        check_vma=False,
    )
```

time: 286 us -> 67.7 us (0.24)
  the two profiles are of different devices: /device:TPU:6 before, /device:TPU:7 now
where the time goes in v2:
time: 67.7 us; the launch traced here: 67.5 us
  Pallas kernels  62.7 us (93%)
  local copies, waits for them, and re-layouts  4.03 us (6%)
  between operations  0.72 us (1%)
    pallas_call x1, Pallas kernels, on_device(): pl.pallas_call(functools.partial(block_kernel, sizes), out_shape=(jax.Sha...  62.7 us
    unnamed x15, local copies, waits for them, and re-layouts  4.03 us

profile of v2, /device:TPU:7, one launch (start us, length us, event | category | flops | bytes accessed | tf_op | source)
XLA Modules:
  0.0 67.5 jit_solution(12589703954423692143)
XLA Ops:
  0.6 0.0 copy-start.2
  0.6 0.0 copy-start.5
  0.7 0.0 copy-start.4
  0.7 0.0 copy-start.3
  0.7 0.9 %copy.9.expand_ref = bf16[256,64]{1,0:T(8,128)(2,1)S(1)} copy(bf16[256,64]{0,1:T(8,128)(2,1)} %param.11) | data formatting | bytes 65536 | tf_op args[4]
  1.6 0.0 copy-done.2
  1.6 0.0 copy-done.5
  1.6 0.0 copy-done.4
  1.6 0.0 copy-done.3
  1.6 0.0 copy-start
  1.6 0.9 %copy-done = bf16[16,16,256]{2,1,0:T(8,128)(2,1)S(1)} copy-done((bf16[16,16,256]{2,1,0:T(8,128)(2,1)S(1)}, bf16[16,16,256]{2,1,0:T(8,128)(2,1)}, u32[]{:S(2)}) %copy-start) | copy-done | bytes 131096
  2.5 0.0 copy-start.1
  2.5 0.9 %copy-done.1 = bf16[16,16,256]{2,1,0:T(8,128)(2,1)S(1)} copy-done((bf16[16,16,256]{2,1,0:T(8,128)(2,1)S(1)}, bf16[16,16,256]{2,1,0:T(8,128)(2,1)}, u32[]{:S(2)}) %copy-start.1) | copy-done | bytes 131096
  3.4 62.7 %ocean_block.1 = (bf16[16,16,256]{2,1,0:T(8,128)(2,1)S(1)}, bf16[16,16,256]{2,1,0:T(8,128)(2,1)S(1)}) custom-call(s32[3072]{0:T(1024)S(1)} %copy-done.4, bf16[16,16,256]{2,1,0:T(8,128)(2,1)S(1)} %copy-done, s32[16,256]{1,0:T(8,128)S(1)} %copy-done.3, bf16[16,49]{1,0:T(8,128)(2,1)S(1)} %copy-done.5, bf16[256,64]{1,0:T(8,128)(2,1)S(1)} %copy.9.expand_ref, ...), custom_call_target="tpu_custom_call" | custom-call | tf_op jit(solution)/shard_map/ocean_block/pallas_call | solution.py:410
  66.1 0.7 copy.12
  66.8 0.7 copy.13
Async XLA Ops:
  0.6 0.9 %copy-start.2 = (bf16[64,256]{1,0:T(8,128)(2,1)S(1)}, bf16[64,256]{1,0:T(8,128)(2,1)}, u32[]{:S(2)}) copy-start(bf16[64,256]{1,0:T(8,128)(2,1)} %project_ref.1) | copy-start | bytes 98308
  0.6 0.9 %copy-start.5 = (bf16[16,49]{1,0:T(8,128)(2,1)S(1)}, bf16[16,49]{1,0:T(8,128)(2,1)}, u32[]{:S(2)}) copy-start(bf16[16,49]{1,0:T(8,128)(2,1)} %kernel_ref.1) | copy-start | bytes 4708
  0.7 0.9 %copy-start.4 = (s32[3072]{0:T(1024)S(1)}, s32[3072]{0:T(1024)}, u32[]{:S(2)}) copy-start(s32[3072]{0:T(1024)} %partner_ref.1) | copy-start | bytes 36868
  0.7 0.9 %copy-start.3 = (s32[16,256]{1,0:T(8,128)S(1)}, s32[16,256]{1,0:T(8,128)}, u32[]{:S(2)}) copy-start(s32[16,256]{1,0:T(8,128)} %mask_ref.1) | copy-start | bytes 49156
  1.6 0.9 %copy-start = (bf16[16,16,256]{2,1,0:T(8,128)(2,1)S(1)}, bf16[16,16,256]{2,1,0:T(8,128)(2,1)}, u32[]{:S(2)}) copy-start(bf16[16,16,256]{2,1,0:T(8,128)(2,1)} %state_ref.1) | copy-start | bytes 393220
  2.5 0.9 %copy-start.1 = (bf16[16,16,256]{2,1,0:T(8,128)(2,1)S(1)}, bf16[16,16,256]{2,1,0:T(8,128)(2,1)}, u32[]{:S(2)}) copy-start(bf16[16,16,256]{2,1,0:T(8,128)(2,1)} %cot_ref.1) | copy-start | bytes 393220

commit v3 on v2

--- a/solution.py
+++ b/solution.py
@@ -31,15 +31,20 @@
 
 def block_kernel(
     sizes,
+    partner_hbm,
+    state_hbm,
+    mask_hbm,
+    kernel_hbm,
+    expand_hbm,
+    project_hbm,
+    cot_hbm,
+    mixed_rows,
+    grad_rows,
     partner_ref,
     state_ref,
     mask_ref,
     kernel_ref,
-    expand_ref,
-    project_ref,
     cot_ref,
-    out_ref,
-    grad_ref,
     ext,
     ext_back,
     fold_rows,
@@ -55,13 +60,15 @@
     normed_ref,
     mixed_send,
     grad_send,
-    mixed_rows,
     halo_send,
     halo_recv,
     halo_send_back,
     halo_recv_back,
     send,
     recv,
+    square_send,
+    square_recv,
+    load,
 ):
     n_lat, n_lon, n_ch, rows, chans, cols, hidden_here = sizes
     wide = cols + 2 * EDGE
@@ -70,6 +77,18 @@
     lat_last = lat == n_lat - 1
     part = lax.rem(lat, 2)
     sibling = lat + 1 - 2 * part
+    pairs = n_lat // 2
+    share = hidden_here // (2 * pairs)
+    mine = pl.ds(pl.multiple_of((lat // 2 * 2 + lax.rem(lon, 2)) * share, share), share)
+    lon_twin = lon + 1 - 2 * lax.rem(lon, 2)
+    square = [(0, 1)] + [(2 * i, j) for i in range(1, pairs) for j in (0, 1)]
+
+    def in_square(turn, flip):
+        return {
+            "lat": lax.rem(lat + turn, n_lat),
+            "lon": lon_twin if flip else lon,
+            "ch": me,
+        }
     own_rows = pl.ds(HALO, rows)
     own_lanes = pl.ds(EDGE, cols)
 
@@ -104,39 +123,46 @@
             pl.semaphore_signal(barrier, device_id=at(dl, do), device_id_type=MESH)
 
     lax.fori_loop(1, n_ch, greet_channel, 0)
+    for turn, flip in square[1:]:
+        pl.semaphore_signal(barrier, device_id=in_square(turn, flip), device_id_type=MESH)
 
     @pl.when(lat_last)
     def _():
         lax.fori_loop(1, n_lon, greet_fold, 0)
+
+    def fetch(k, src, dst):
+        return pltpu.make_async_copy(src, dst, load.at[k])
+
+    loads = [
+        fetch(0, state_hbm, state_ref),
+        fetch(1, mask_hbm, mask_ref),
+        fetch(2, kernel_hbm, kernel_ref),
+        fetch(3, cot_hbm, cot_ref),
+        fetch(4, partner_hbm, partner_ref),
+    ]
+    own_expand = fetch(5, expand_hbm.at[mine], weights.at[0, me, mine])
+    own_project = fetch(5, project_hbm.at[mine], weights.at[1, me, mine])
+    for copy in loads:
+        copy.start()
+
+    @pl.when(part == 0)
+    def _():
+        own_expand.start()
+
+    @pl.when(part == 1)
+    def _():
+        own_project.start()
 
     swap_row = lax.broadcasted_iota(jnp.int32, (cells, cells), 0)
     swap_col = lax.broadcasted_iota(jnp.int32, (cells, cells), 1)
     to_rows = (swap_col == lax.rem(swap_row, chans) * rows + swap_row // chans).astype(BF16)
+    loads[0].wait()
+    loads[1].wait()
     mask_half = mask_ref[...].astype(BF16)
     masked = (state_ref[...] * mask_half[None]).reshape(cells, cols)
     ext[own_rows, :, own_lanes] = (
         dot(to_rows, masked).astype(BF16).reshape(rows, chans, cols)
     )
-    masked_cot = (cot_ref[...] * mask_half[None]).reshape(cells, cols)
-    cot_rows[...] = dot(to_rows, masked_cot).astype(BF16).reshape(rows, chans, cols)
-    cot_all[me] = cot_rows[me]
-
-    @pl.when(part == 0)
-    def _():
-        unit_row = lax.broadcasted_iota(jnp.int32, (n_ch * chans, n_ch * chans), 0)
-        unit_col = lax.broadcasted_iota(jnp.int32, (n_ch * chans, n_ch * chans), 1)
-        unit = (unit_row == unit_col).astype(BF16)
-        weights[0, me] = dot(expand_ref[...], unit, ((0,), (0,))).astype(BF16)
-
-    @pl.when(part == 1)
-    def _():
-        weights[1, me] = project_ref[...]
-
-    for t in range(TAPS * TAPS):
-        tap = jnp.broadcast_to(kernel_ref[:, t : t + 1].astype(F32), (chans, EDGE))
-        taps[0, t] = tap
-        taps[1, TAPS * TAPS - 1 - t] = tap
-
     @pl.when(lat == 0)
     def _():
         ext[0:HALO] = jnp.zeros((HALO, chans, wide), BF16)
@@ -146,8 +172,9 @@
     def _():
         fold_rows[lon] = ext[pl.ds(rows, HALO), :, own_lanes]
 
+    own_expand.wait()
     neighbours = sum(
-        (exists(dl).astype(jnp.int32) for dl, _ in DIRECTIONS), jnp.int32(n_ch - 1)
+        (exists(dl).astype(jnp.int32) for dl, _ in DIRECTIONS), jnp.int32(n_ch - 1 + len(square) - 1)
     ) + jnp.where(lat_last, n_lon - 1, 0)
     pl.semaphore_wait(barrier, neighbours)
 
@@ -237,9 +264,22 @@
     def _():
         fold_start(ext, fold_rows, 0)
 
-    own_weights = weights.at[part, me]
+    own_weights = weights.at[part, me, mine]
     channel_copies(lambda peer: own_weights, lambda: own_weights, 1)
+
+    loads[3].wait()
+    masked_cot = (cot_ref[...] * mask_half[None]).reshape(cells, cols)
+    cot_rows[...] = dot(to_rows, masked_cot).astype(BF16).reshape(rows, chans, cols)
     channel_copies(lambda peer: cot_rows.at[peer], lambda: cot_all.at[me], 2)
+    cot_all[me] = cot_rows[me]
+
+    loads[2].wait()
+    for t in range(TAPS * TAPS):
+        tap = jnp.broadcast_to(kernel_ref[:, t : t + 1].astype(F32), (chans, EDGE))
+        taps[0, t] = tap
+        taps[1, TAPS * TAPS - 1 - t] = tap
+
+    loads[4].wait()
 
     full_width = n_lon * cols
     turn = partner_ref[0]
@@ -263,11 +303,8 @@
         for j in range(HALO):
             buffer[HALO + rows + j] = found[HALO - 1 - j]
 
-    def conv(buffer, table_of):
-        acc[...] = jnp.zeros(acc.shape, F32)
-
+    def conv(buffer, table, start, stop):
         def step(e, carry):
-            table = table_of(e)
             line = buffer[e].astype(F32)
             shifted = [
                 line[:, EDGE - HALO + b : EDGE - HALO + b + cols] for b in range(TAPS)
@@ -280,32 +317,52 @@
                 acc[e - a + TAPS - 1] = total
             return carry
 
-        lax.fori_loop(0, rows + 2 * HALO, step, 0)
-
+        lax.fori_loop(start, stop, step, 0)
+
+    def square_copy(k):
+        turn, flip = square[k]
+        piece = weights.at[part, :, mine]
+        return pltpu.make_async_remote_copy(
+            src_ref=piece,
+            dst_ref=piece,
+            send_sem=square_send.at[k],
+            recv_sem=square_recv.at[k],
+            device_id=in_square(turn, flip),
+            device_id_type=MESH,
+        )
+
+    last_rows = HALO + rows
+    acc[...] = jnp.zeros(acc.shape, F32)
     halo_arrived(ext, halo_send, halo_recv)
+    several(weights.at[part, :, mine], n_ch - 1, 1).wait_recv()
+    for k in range(len(square)):
+        square_copy(k).start()
+    conv(ext, 0, 0, last_rows)
 
     @pl.when(lat_last)
     def _():
         several(fold_rows, n_lon - 1, 0).wait_recv()
         fold_fill(ext, fold_rows)
 
-    conv(ext, lambda e: 0)
+    conv(ext, 0, last_rows, last_rows + HALO)
     depth_rows[...] = acc[pl.ds(TAPS - 1, rows)].astype(BF16)
     channel_copies(lambda peer: depth_rows.at[peer], lambda: depth_all.at[me], 3)
     depth_all[me] = depth_rows[me]
-
-    def swap_weights():
+    acc[...] = jnp.zeros(acc.shape, F32)
+
+    def swap_weights(half):
         return pltpu.make_async_remote_copy(
-            src_ref=weights.at[part],
-            dst_ref=weights.at[part],
+            src_ref=weights.at[half],
+            dst_ref=weights.at[half],
             send_sem=send.at[4],
             recv_sem=recv.at[4],
             device_id={"lat": sibling, "lon": lon, "ch": me},
             device_id_type=MESH,
         )
 
-    several(weights.at[part], n_ch - 1, 1).wait_recv()
-    swap_weights().start()
+    for k in range(len(square)):
+        square_copy(k).wait_recv()
+    swap_weights(part).start()
     several(cot_all, n_ch - 1, 2).wait_recv()
     several(depth_all, n_ch - 1, 3).wait_recv()
 
@@ -316,14 +373,7 @@
     normed_ref[...] = spread * inv_scale
     normed_half = normed_ref[...].astype(BF16)
     cot_here = cot_all[...].reshape(channels, cols)
-    pltpu.make_async_remote_copy(
-        src_ref=weights.at[1 - part],
-        dst_ref=weights.at[1 - part],
-        send_sem=send.at[4],
-        recv_sem=recv.at[4],
-        device_id={"lat": sibling, "lon": lon, "ch": me},
-        device_id_type=MESH,
-    ).wait_recv()
+    swap_weights(1 - part).wait_recv()
 
     mixed = jnp.zeros((channels, cols), F32)
     back_norm = jnp.zeros((channels, cols), F32)
@@ -359,27 +409,20 @@
         fold_start(ext_back, fold_rows_back, 7)
         fold_rows_back[lon] = ext_back[pl.ds(rows, HALO), :, own_lanes]
 
-    several(mixed_rows, n_ch - 1, 6).wait_recv()
-    to_chans = (swap_col == lax.rem(swap_row, rows) * chans + swap_row // rows).astype(BF16)
-    mixed_here = dot(to_chans, mixed_rows[...].reshape(cells, cols)).reshape(chans, rows, cols)
-    ocean = mask_ref[...].astype(F32)
-    out_ref[...] = (ocean[None] * (state_ref[...].astype(F32) + mixed_here)).astype(BF16)
-
     halo_arrived(ext_back, halo_send_back, halo_recv_back)
+    conv(ext_back, 1, 0, last_rows)
 
     @pl.when(lat_last)
     def _():
         several(fold_rows_back, n_lon - 1, 7).wait_recv()
         fold_fill(ext_back, fold_rows_back)
 
-    fold_from = jnp.where(lat_last, HALO + rows, rows + 2 * HALO)
-    conv(ext_back, lambda e: jnp.where(e >= fold_from, 0, 1))
-    grad_rows = (
+    conv(ext_back, jnp.where(lat_last, 0, 1), last_rows, last_rows + HALO)
+    ocean = mask_ref[...].astype(F32)
+    grad_rows[...] = (
         cot_rows[...].astype(F32) + ocean[:, None, :] * acc[pl.ds(TAPS - 1, rows)]
     ).astype(BF16)
-    grad_ref[...] = (
-        dot(to_chans, grad_rows.reshape(cells, cols)).astype(BF16).reshape(chans, rows, cols)
-    )
+    several(mixed_rows, n_ch - 1, 6).wait_recv()
 
     halo_sent(ext, halo_send, halo_recv)
     halo_sent(ext_back, halo_send_back, halo_recv_back)
@@ -389,12 +432,30 @@
         several(fold_rows, n_lon - 1, 0).wait_send()
         several(fold_rows_back, n_lon - 1, 7).wait_send()
 
-    several(weights.at[part], n_ch - 1, 1).wait_send()
+    several(weights.at[part, :, mine], n_ch - 1, 1).wait_send()
+    for k in range(len(square)):
+        square_copy(k).wait_send()
     several(cot_rows, n_ch - 1, 2).wait_send()
     several(depth_rows, n_ch - 1, 3).wait_send()
-    swap_weights().wait_send()
+    swap_weights(part).wait_send()
     several(grad_send, n_ch - 1, 5).wait_send()
     several(mixed_send, n_ch - 1, 6).wait_send()
+
+
+def finish_kernel(state_ref, mask_ref, mixed_rows, grad_rows, out_ref, grad_ref):
+    chans, rows, cols = state_ref.shape
+    cells = rows * chans
+    swap_row = lax.broadcasted_iota(jnp.int32, (cells, cells), 0)
+    swap_col = lax.broadcasted_iota(jnp.int32, (cells, cells), 1)
+    to_chans = (swap_col == lax.rem(swap_row, rows) * chans + swap_row // rows).astype(BF16)
+    mixed = dot(to_chans, mixed_rows[...].reshape(cells, cols)).reshape(chans, rows, cols)
+    ocean = mask_ref[...].astype(F32)
+    out_ref[...] = (ocean[None] * (state_ref[...].astype(F32) + mixed)).astype(BF16)
+    grad_ref[...] = (
+        dot(to_chans, grad_rows[...].reshape(cells, cols))
+        .astype(BF16)
+        .reshape(chans, rows, cols)
+    )
 
 
 def on_device(state_field, land_mask, partner, kernel, w_expand, w_project, cotangent):
@@ -407,12 +468,18 @@
     sizes = (n_lat, n_lon, n_ch, rows, chans, cols, hidden_here)
     vmem = pl.BlockSpec(memory_space=pltpu.VMEM)
     tile_rows = rows + 2 * HALO
-    return pl.pallas_call(
+    by_row = jax.ShapeDtypeStruct((rows, chans, cols), BF16)
+    mixed_rows, grad_rows = pl.pallas_call(
         functools.partial(block_kernel, sizes),
-        out_shape=(jax.ShapeDtypeStruct(state_field.shape, BF16),) * 2,
-        in_specs=[pl.BlockSpec(memory_space=pltpu.SMEM)] + [vmem] * 6,
+        out_shape=(by_row, by_row),
+        in_specs=[pl.BlockSpec(memory_space=pltpu.HBM)] * 7,
         out_specs=(vmem, vmem),
         scratch_shapes=[
+            pltpu.SMEM(partner.shape, jnp.int32),
+            pltpu.VMEM(state_field.shape, BF16),
+            pltpu.VMEM(land_mask.shape, jnp.int32),
+            pltpu.VMEM(kernel.shape, BF16),
+            pltpu.VMEM(cotangent.shape, BF16),
             pltpu.VMEM((tile_rows, chans, wide), BF16),
             pltpu.VMEM((tile_rows, chans, wide), BF16),
             pltpu.VMEM((n_lon, HALO, chans, cols), BF16),
@@ -428,19 +495,28 @@
             pltpu.VMEM((channels, cols), F32),
             pltpu.VMEM((n_ch, chans, cols), BF16),
             pltpu.VMEM((n_ch, chans, cols), BF16),
-            pltpu.VMEM((n_ch, chans, cols), BF16),
             pltpu.SemaphoreType.DMA((8,)),
             pltpu.SemaphoreType.DMA((8,)),
             pltpu.SemaphoreType.DMA((8,)),
             pltpu.SemaphoreType.DMA((8,)),
             pltpu.SemaphoreType.DMA((8,)),
             pltpu.SemaphoreType.DMA((8,)),
+            pltpu.SemaphoreType.DMA((n_lat - 1,)),
+            pltpu.SemaphoreType.DMA((n_lat - 1,)),
+            pltpu.SemaphoreType.DMA((6,)),
         ],
         compiler_params=pltpu.CompilerParams(
-            collective_id=0, has_side_effects=True, vmem_limit_bytes=48 * 1024 * 1024
+            collective_id=0, has_side_effects=True, vmem_limit_bytes=64 * 1000 * 1000
         ),
         name="ocean_block",
-    )(partner, state_field, land_mask, kernel, w_expand, w_project, cotangent)
+    )(partner, state_field, land_mask, kernel, w_expand.T, w_project, cotangent)
+    return pl.pallas_call(
+        finish_kernel,
+        out_shape=(jax.ShapeDtypeStruct(state_field.shape, BF16),) * 2,
+        in_specs=[vmem] * 4,
+        out_specs=(vmem, vmem),
+        name="finish",
+    )(state_field, land_mask, mixed_rows, grad_rows)
 
 
 def solution(mesh):

time: 67.7 us -> 60.3 us (0.89)
  local copies, waits for them, and re-layouts: 4.03 us -> 0 us
  Pallas kernels: 62.7 us -> 58.9 us
    unnamed x15 -> x0, local copies, waits for them, and re-layouts: 4.03 us -> none
    pallas_call x1 -> x2, Pallas kernels: 62.7 us -> 58.9 us  [the longest x1 56.9 us: on_device(): pl.pallas_call(functools.partial(block_kernel, sizes), out_shape=(by_row,...]
where the time goes in v3:
time: 60.3 us; the launch traced here: 59.5 us
  Pallas kernels  58.9 us (98%)
  between operations  0.64 us (1%)
    pallas_call x1, Pallas kernels, on_device(): pl.pallas_call(functools.partial(block_kernel, sizes), out_shape=(by_row,...  56.9 us
    pallas_call x1, Pallas kernels, on_device(): pl.pallas_call(finish_kernel, out_shape=(jax.ShapeDtypeStruct(state_field...  1.98 us

profile of v3, /device:TPU:7, one launch (start us, length us, event | category | flops | bytes accessed | tf_op | source)
XLA Modules:
  0.0 59.5 jit_solution(2804567966411763315)
XLA Ops:
  0.6 56.9 %ocean_block.1 = (bf16[16,16,256]{2,1,0:T(8,128)(2,1)}, bf16[16,16,256]{2,1,0:T(8,128)(2,1)}) custom-call(s32[3072]{0:T(1024)} %partner_hbm.1, bf16[16,16,256]{2,1,0:T(8,128)(2,1)} %state_ref.1, s32[16,256]{1,0:T(8,128)} %mask_ref.1, bf16[16,49]{1,0:T(8,128)(2,1)} %kernel_hbm.1, bf16[64,256]{1,0:T(8,128)(2,1)} %bitcast.1, bf16[64,256]{1,0:T(8,128)(2,1)} %project_hbm.1, ...), custom_call_target="tpu_custom_call" | custom-call | tf_op jit(solution)/shard_map/ocean_block/pallas_call | solution.py:472
  57.5 2.0 %finish.1 = (bf16[16,16,256]{2,1,0:T(8,128)(2,1)}, bf16[16,16,256]{2,1,0:T(8,128)(2,1)}) custom-call(bf16[16,16,256]{2,1,0:T(8,128)(2,1)} %state_ref.1, s32[16,256]{1,0:T(8,128)} %mask_ref.1, bf16[16,16,256]{2,1,0:T(8,128)(2,1)} %get-tuple-element.4.mixed_rows, bf16[16,16,256]{2,1,0:T(8,128)(2,1)} %get-tuple-element.5.grad_rows), custom_call_target="tpu_custom_call" | custom-call | tf_op jit(solution)/shard_map/finish/pallas_call | solution.py:513

commit v4 on v3

--- a/solution.py
+++ b/solution.py
@@ -38,8 +38,8 @@
     expand_hbm,
     project_hbm,
     cot_hbm,
-    mixed_rows,
-    grad_rows,
+    state_sum,
+    grad_sum,
     partner_ref,
     state_ref,
     mask_ref,
@@ -52,14 +52,18 @@
     pick,
     taps,
     acc,
+    edge_taps,
+    edge_acc,
     cot_rows,
     cot_all,
     depth_rows,
     depth_all,
     weights,
+    weights_send,
     normed_ref,
     mixed_send,
     grad_send,
+    mixed_rows,
     halo_send,
     halo_recv,
     halo_send_back,
@@ -79,7 +83,13 @@
     sibling = lat + 1 - 2 * part
     pairs = n_lat // 2
     share = hidden_here // (2 * pairs)
-    mine = pl.ds(pl.multiple_of((lat // 2 * 2 + lax.rem(lon, 2)) * share, share), share)
+    across = lax.rem(lat + pairs, n_lat)
+
+    def share_of(row_block):
+        index = row_block // 2 * 2 + lax.rem(lon, 2)
+        return pl.ds(pl.multiple_of(index * share, share), share)
+
+    mine, given = share_of(across), share_of(lat)
     lon_twin = lon + 1 - 2 * lax.rem(lon, 2)
     square = [(0, 1)] + [(2 * i, j) for i in range(1, pairs) for j in (0, 1)]
 
@@ -103,7 +113,7 @@
     def greet_channel(i, carry):
         pl.semaphore_signal(
             barrier,
-            device_id={"lat": lat, "lon": lon, "ch": lax.rem(me + i, n_ch)},
+            device_id={"lat": across, "lon": lon, "ch": i},
             device_id_type=MESH,
         )
         return carry
@@ -122,8 +132,10 @@
         def _():
             pl.semaphore_signal(barrier, device_id=at(dl, do), device_id_type=MESH)
 
-    lax.fori_loop(1, n_ch, greet_channel, 0)
+    lax.fori_loop(0, n_ch, greet_channel, 0)
     for turn, flip in square[1:]:
+        if (turn, flip) == (pairs, 0):
+            continue
         pl.semaphore_signal(barrier, device_id=in_square(turn, flip), device_id_type=MESH)
 
     @pl.when(lat_last)
@@ -140,18 +152,26 @@
         fetch(3, cot_hbm, cot_ref),
         fetch(4, partner_hbm, partner_ref),
     ]
-    own_expand = fetch(5, expand_hbm.at[mine], weights.at[0, me, mine])
-    own_project = fetch(5, project_hbm.at[mine], weights.at[1, me, mine])
+    own_expand = [
+        fetch(5, expand_hbm.at[mine], weights.at[0, me, mine]),
+        fetch(6, expand_hbm.at[given], weights_send),
+    ]
+    own_project = [
+        fetch(5, project_hbm.at[mine], weights.at[1, me, mine]),
+        fetch(6, project_hbm.at[given], weights_send),
+    ]
     for copy in loads:
         copy.start()
 
     @pl.when(part == 0)
     def _():
-        own_expand.start()
+        for copy in own_expand:
+            copy.start()
 
     @pl.when(part == 1)
     def _():
-        own_project.start()
+        for copy in own_project:
+            copy.start()
 
     swap_row = lax.broadcasted_iota(jnp.int32, (cells, cells), 0)
     swap_col = lax.broadcasted_iota(jnp.int32, (cells, cells), 1)
@@ -172,9 +192,10 @@
     def _():
         fold_rows[lon] = ext[pl.ds(rows, HALO), :, own_lanes]
 
-    own_expand.wait()
+    for copy in own_expand:
+        copy.wait()
     neighbours = sum(
-        (exists(dl).astype(jnp.int32) for dl, _ in DIRECTIONS), jnp.int32(n_ch - 1 + len(square) - 1)
+        (exists(dl).astype(jnp.int32) for dl, _ in DIRECTIONS), jnp.int32(n_ch + len(square) - 2)
     ) + jnp.where(lat_last, n_lon - 1, 0)
     pl.semaphore_wait(barrier, neighbours)
 
@@ -232,24 +253,32 @@
             dst_ref=whole,
             send_sem=send.at[k],
             recv_sem=recv.at[k],
-            device_id={"lat": lat, "lon": lon, "ch": lax.rem(me + 1, n_ch)},
+            device_id={"lat": across, "lon": lon, "ch": me},
             device_id_type=MESH,
         )
 
-    def channel_copies(make_src, make_dst, k):
-        def step(i, carry):
-            peer = lax.rem(me + i, n_ch)
-            pltpu.make_async_remote_copy(
-                src_ref=make_src(peer),
-                dst_ref=make_dst(),
-                send_sem=send.at[k],
-                recv_sem=recv.at[k],
-                device_id={"lat": lat, "lon": lon, "ch": peer},
-                device_id_type=MESH,
-            ).start()
+    def channel_copies(make_src, dst, k, wanted=None):
+        def step(j, carry):
+            away = (j + 1) // 2
+            peer = lax.rem(me + n_ch // 2 + n_ch + away * (1 - 2 * lax.rem(j, 2)), n_ch)
+
+            def go():
+                pltpu.make_async_remote_copy(
+                    src_ref=make_src(peer),
+                    dst_ref=dst,
+                    send_sem=send.at[k],
+                    recv_sem=recv.at[k],
+                    device_id={"lat": across, "lon": lon, "ch": peer},
+                    device_id_type=MESH,
+                ).start()
+
+            if wanted is None:
+                go()
+            else:
+                pl.when(wanted(peer))(go)
             return carry
 
-        lax.fori_loop(1, n_ch, step, 0)
+        lax.fori_loop(0, n_ch, step, 0)
 
     def fold_start(buffer, gathered, k):
         def step(i, carry):
@@ -264,20 +293,97 @@
     def _():
         fold_start(ext, fold_rows, 0)
 
-    own_weights = weights.at[part, me, mine]
-    channel_copies(lambda peer: own_weights, lambda: own_weights, 1)
-
-    loads[3].wait()
-    masked_cot = (cot_ref[...] * mask_half[None]).reshape(cells, cols)
-    cot_rows[...] = dot(to_rows, masked_cot).astype(BF16).reshape(rows, chans, cols)
-    channel_copies(lambda peer: cot_rows.at[peer], lambda: cot_all.at[me], 2)
-    cot_all[me] = cot_rows[me]
-
+    channel_copies(
+        lambda peer: weights_send, weights.at[part, me, given], 1, lambda peer: peer != me
+    )
     loads[2].wait()
     for t in range(TAPS * TAPS):
         tap = jnp.broadcast_to(kernel_ref[:, t : t + 1].astype(F32), (chans, EDGE))
         taps[0, t] = tap
         taps[1, TAPS * TAPS - 1 - t] = tap
+    lane = lax.broadcasted_iota(jnp.int32, (chans, EDGE), 1)
+    for table in range(2):
+        for a in range(TAPS):
+            for b in range(HALO):
+                edge_taps[table, a * HALO + b] = jnp.where(
+                    lane < EDGE // 2,
+                    taps[table, a * TAPS + b],
+                    taps[table, a * TAPS + b + HALO + 1],
+                )
+
+    def add_line(line, table, e, a):
+        parts = [
+            jnp.concatenate([taps[table, a * TAPS + b]] * (cols // EDGE), axis=1)
+            * line[:, EDGE - HALO + b : EDGE - HALO + b + cols]
+            for b in range(TAPS)
+        ]
+        acc[e - a + TAPS - 1] += ((parts[0] + parts[1]) + (parts[2] + parts[3])) + (
+            (parts[4] + parts[5]) + parts[6]
+        )
+
+    def conv_own(buffer, table):
+        acc[...] = jnp.zeros(acc.shape, F32)
+        edge_acc[...] = jnp.zeros(edge_acc.shape, F32)
+        blank = jnp.zeros((chans, EDGE), F32)
+
+        def step(e, carry):
+            own = buffer[e, :, own_lanes].astype(F32)
+            line = jnp.concatenate([blank, own, blank], axis=1)
+            for a in range(TAPS):
+                add_line(line, table, e, a)
+            return carry
+
+        lax.fori_loop(HALO, HALO + rows, step, 0, unroll=2)
+
+    def conv_edges(buffer, table):
+        def step(e, carry):
+            left = jnp.where(lane >= EDGE // 2, buffer[e, :, pl.ds(0, EDGE)].astype(F32), 0.0)
+            right = jnp.where(
+                lane < EDGE // 2, buffer[e, :, pl.ds(EDGE + cols, EDGE)].astype(F32), 0.0
+            )
+            moved = [
+                jnp.where(
+                    lane < EDGE // 2,
+                    pltpu.roll(left, HALO - b, 1),
+                    pltpu.roll(right, EDGE - 1 - b, 1),
+                )
+                for b in range(HALO)
+            ]
+            for a in range(TAPS):
+                parts = [edge_taps[table, a * HALO + b] * moved[b] for b in range(HALO)]
+                edge_acc[e - a + TAPS - 1] += (parts[0] + parts[1]) + parts[2]
+            return carry
+
+        lax.fori_loop(HALO, HALO + rows, step, 0, unroll=2)
+
+    def conv_outer(buffer, table, lines):
+        for e in lines:
+            line = buffer[e].astype(F32)
+            for a in range(TAPS):
+                if 0 <= e - a < rows:
+                    add_line(line, table, e, a)
+
+    def conv_total(start, count):
+        edge = edge_acc[pl.ds(TAPS - 1 + start, count)]
+        both = jnp.concatenate(
+            [
+                jnp.where(lane < EDGE // 2, edge, 0.0),
+                jnp.zeros((count, chans, cols - 2 * EDGE), F32),
+                jnp.where(lane < EDGE // 2, 0.0, edge),
+            ][:: 1 if cols > 2 * EDGE else 2],
+            axis=2,
+        )
+        return acc[pl.ds(TAPS - 1 + start, count)] + both
+
+    below, above = range(HALO), range(HALO + rows, HALO + rows + HALO)
+    settled = rows - HALO
+
+    conv_own(ext, 0)
+
+    loads[3].wait()
+    masked_cot = (cot_ref[...] * mask_half[None]).reshape(cells, cols)
+    cot_rows[...] = dot(to_rows, masked_cot).astype(BF16).reshape(rows, chans, cols)
+    channel_copies(lambda peer: cot_rows.at[peer], cot_all.at[me], 2)
 
     loads[4].wait()
 
@@ -302,22 +408,6 @@
         found = found.astype(BF16).reshape(HALO, chans, wide)
         for j in range(HALO):
             buffer[HALO + rows + j] = found[HALO - 1 - j]
-
-    def conv(buffer, table, start, stop):
-        def step(e, carry):
-            line = buffer[e].astype(F32)
-            shifted = [
-                line[:, EDGE - HALO + b : EDGE - HALO + b + cols] for b in range(TAPS)
-            ]
-            for a in range(TAPS):
-                total = acc[e - a + TAPS - 1]
-                for b in range(TAPS):
-                    tap = taps[table, a * TAPS + b]
-                    total = total + jnp.concatenate([tap] * (cols // EDGE), axis=1) * shifted[b]
-                acc[e - a + TAPS - 1] = total
-            return carry
-
-        lax.fori_loop(start, stop, step, 0)
 
     def square_copy(k):
         turn, flip = square[k]
@@ -331,24 +421,27 @@
             device_id_type=MESH,
         )
 
-    last_rows = HALO + rows
-    acc[...] = jnp.zeros(acc.shape, F32)
-    halo_arrived(ext, halo_send, halo_recv)
     several(weights.at[part, :, mine], n_ch - 1, 1).wait_recv()
     for k in range(len(square)):
         square_copy(k).start()
-    conv(ext, 0, 0, last_rows)
+    halo_arrived(ext, halo_send, halo_recv)
+    conv_edges(ext, 0)
+    conv_outer(ext, 0, below)
+    depth_rows[pl.ds(0, settled)] = conv_total(0, settled).astype(BF16)
+    channel_copies(
+        lambda peer: depth_rows.at[peer], depth_all.at[me], 3, lambda peer: peer < settled
+    )
 
     @pl.when(lat_last)
     def _():
         several(fold_rows, n_lon - 1, 0).wait_recv()
         fold_fill(ext, fold_rows)
 
-    conv(ext, 0, last_rows, last_rows + HALO)
-    depth_rows[...] = acc[pl.ds(TAPS - 1, rows)].astype(BF16)
-    channel_copies(lambda peer: depth_rows.at[peer], lambda: depth_all.at[me], 3)
-    depth_all[me] = depth_rows[me]
-    acc[...] = jnp.zeros(acc.shape, F32)
+    conv_outer(ext, 0, above)
+    depth_rows[pl.ds(settled, HALO)] = conv_total(settled, HALO).astype(BF16)
+    channel_copies(
+        lambda peer: depth_rows.at[peer], depth_all.at[me], 3, lambda peer: peer >= settled
+    )
 
     def swap_weights(half):
         return pltpu.make_async_remote_copy(
@@ -363,8 +456,8 @@
     for k in range(len(square)):
         square_copy(k).wait_recv()
     swap_weights(part).start()
-    several(cot_all, n_ch - 1, 2).wait_recv()
-    several(depth_all, n_ch - 1, 3).wait_recv()
+    several(cot_all, n_ch, 2).wait_recv()
+    several(depth_all, n_ch, 3).wait_recv()
 
     channels = n_ch * chans
     values = depth_all[...].reshape(channels, cols).astype(F32)
@@ -394,14 +487,11 @@
         .astype(BF16)
         .reshape(n_ch, chans, cols)
     )
-    back_row = ext_back.at[HALO + me, :, own_lanes]
-    channel_copies(lambda peer: grad_send.at[peer], lambda: back_row, 5)
-    ext_back[HALO + me, :, own_lanes] = grad_send[me]
+    channel_copies(lambda peer: grad_send.at[peer], ext_back.at[HALO + me, :, own_lanes], 5)
     mixed_send[...] = mixed.astype(BF16).reshape(n_ch, chans, cols)
-    channel_copies(lambda peer: mixed_send.at[peer], lambda: mixed_rows.at[me], 6)
-    mixed_rows[me] = mixed_send[me]
-
-    several(grad_send, n_ch - 1, 5).wait_recv()
+    channel_copies(lambda peer: mixed_send.at[peer], mixed_rows.at[me], 6)
+
+    several(grad_send, n_ch, 5).wait_recv()
     halo_start(ext_back, halo_send_back, halo_recv_back)
 
     @pl.when(lat_last)
@@ -409,20 +499,29 @@
         fold_start(ext_back, fold_rows_back, 7)
         fold_rows_back[lon] = ext_back[pl.ds(rows, HALO), :, own_lanes]
 
+    conv_own(ext_back, 1)
+    to_chans = (swap_col == lax.rem(swap_row, rows) * chans + swap_row // rows).astype(BF16)
+    several(mixed_rows, n_ch, 6).wait_recv()
+    mixed_here = dot(to_chans, mixed_rows[...].reshape(cells, cols)).reshape(chans, rows, cols)
+    state_sum[...] = (state_ref[...].astype(F32) + mixed_here).astype(BF16)
+
     halo_arrived(ext_back, halo_send_back, halo_recv_back)
-    conv(ext_back, 1, 0, last_rows)
+    conv_edges(ext_back, 1)
+    conv_outer(ext_back, 1, below)
 
     @pl.when(lat_last)
     def _():
         several(fold_rows_back, n_lon - 1, 7).wait_recv()
         fold_fill(ext_back, fold_rows_back)
 
-    conv(ext_back, jnp.where(lat_last, 0, 1), last_rows, last_rows + HALO)
+    conv_outer(ext_back, jnp.where(lat_last, 0, 1), above)
     ocean = mask_ref[...].astype(F32)
-    grad_rows[...] = (
-        cot_rows[...].astype(F32) + ocean[:, None, :] * acc[pl.ds(TAPS - 1, rows)]
+    grad_rows = (
+        cot_rows[...].astype(F32) + ocean[:, None, :] * conv_total(0, rows)
     ).astype(BF16)
-    several(mixed_rows, n_ch - 1, 6).wait_recv()
+    grad_sum[...] = (
+        dot(to_chans, grad_rows.reshape(cells, cols)).astype(BF16).reshape(chans, rows, cols)
+    )
 
     halo_sent(ext, halo_send, halo_recv)
     halo_sent(ext_back, halo_send_back, halo_recv_back)
@@ -435,27 +534,11 @@
     several(weights.at[part, :, mine], n_ch - 1, 1).wait_send()
     for k in range(len(square)):
         square_copy(k).wait_send()
-    several(cot_rows, n_ch - 1, 2).wait_send()
-    several(depth_rows, n_ch - 1, 3).wait_send()
+    several(cot_rows, n_ch, 2).wait_send()
+    several(depth_rows, n_ch, 3).wait_send()
     swap_weights(part).wait_send()
-    several(grad_send, n_ch - 1, 5).wait_send()
-    several(mixed_send, n_ch - 1, 6).wait_send()
-
-
-def finish_kernel(state_ref, mask_ref, mixed_rows, grad_rows, out_ref, grad_ref):
-    chans, rows, cols = state_ref.shape
-    cells = rows * chans
-    swap_row = lax.broadcasted_iota(jnp.int32, (cells, cells), 0)
-    swap_col = lax.broadcasted_iota(jnp.int32, (cells, cells), 1)
-    to_chans = (swap_col == lax.rem(swap_row, rows) * chans + swap_row // rows).astype(BF16)
-    mixed = dot(to_chans, mixed_rows[...].reshape(cells, cols)).reshape(chans, rows, cols)
-    ocean = mask_ref[...].astype(F32)
-    out_ref[...] = (ocean[None] * (state_ref[...].astype(F32) + mixed)).astype(BF16)
-    grad_ref[...] = (
-        dot(to_chans, grad_rows[...].reshape(cells, cols))
-        .astype(BF16)
-        .reshape(chans, rows, cols)
-    )
+    several(grad_send, n_ch, 5).wait_send()
+    several(mixed_send, n_ch, 6).wait_send()
 
 
 def on_device(state_field, land_mask, partner, kernel, w_expand, w_project, cotangent):
@@ -468,10 +551,9 @@
     sizes = (n_lat, n_lon, n_ch, rows, chans, cols, hidden_here)
     vmem = pl.BlockSpec(memory_space=pltpu.VMEM)
     tile_rows = rows + 2 * HALO
-    by_row = jax.ShapeDtypeStruct((rows, chans, cols), BF16)
-    mixed_rows, grad_rows = pl.pallas_call(
+    state_sum, grad_sum = pl.pallas_call(
         functools.partial(block_kernel, sizes),
-        out_shape=(by_row, by_row),
+        out_shape=(jax.ShapeDtypeStruct(state_field.shape, BF16),) * 2,
         in_specs=[pl.BlockSpec(memory_space=pltpu.HBM)] * 7,
         out_specs=(vmem, vmem),
         scratch_shapes=[
@@ -487,12 +569,16 @@
             pltpu.VMEM((3 * cols, wide), BF16),
             pltpu.VMEM((2, TAPS * TAPS, chans, EDGE), F32),
             pltpu.VMEM((rows + 2 * (TAPS - 1), chans, cols), F32),
+            pltpu.VMEM((2, TAPS * HALO, chans, EDGE), F32),
+            pltpu.VMEM((rows + 2 * (TAPS - 1), chans, EDGE), F32),
             pltpu.VMEM((rows, chans, cols), BF16),
             pltpu.VMEM((n_ch, chans, cols), BF16),
             pltpu.VMEM((rows, chans, cols), BF16),
             pltpu.VMEM((n_ch, chans, cols), BF16),
             pltpu.VMEM((2, n_ch, hidden_here, channels), BF16),
+            pltpu.VMEM((hidden_here // n_lat, channels), BF16),
             pltpu.VMEM((channels, cols), F32),
+            pltpu.VMEM((n_ch, chans, cols), BF16),
             pltpu.VMEM((n_ch, chans, cols), BF16),
             pltpu.VMEM((n_ch, chans, cols), BF16),
             pltpu.SemaphoreType.DMA((8,)),
@@ -503,20 +589,15 @@
             pltpu.SemaphoreType.DMA((8,)),
             pltpu.SemaphoreType.DMA((n_lat - 1,)),
             pltpu.SemaphoreType.DMA((n_lat - 1,)),
-            pltpu.SemaphoreType.DMA((6,)),
+            pltpu.SemaphoreType.DMA((7,)),
         ],
         compiler_params=pltpu.CompilerParams(
             collective_id=0, has_side_effects=True, vmem_limit_bytes=64 * 1000 * 1000
         ),
         name="ocean_block",
     )(partner, state_field, land_mask, kernel, w_expand.T, w_project, cotangent)
-    return pl.pallas_call(
-        finish_kernel,
-        out_shape=(jax.ShapeDtypeStruct(state_field.shape, BF16),) * 2,
-        in_specs=[vmem] * 4,
-        out_specs=(vmem, vmem),
-        name="finish",
-    )(state_field, land_mask, mixed_rows, grad_rows)
+    mask_half = land_mask.astype(BF16)[None]
+    return (state_sum * mask_half, grad_sum * mask_half)
 
 
 def solution(mesh):

time: 60.3 us -> 56.7 us (0.940)
  Pallas kernels: 58.9 us -> 53 us
  other arithmetic: 0 us -> 2.41 us
    pallas_call x2 -> x1, Pallas kernels: 58.9 us -> 53 us  [on_device(): pl.pallas_call(functools.partial(block_kernel, sizes), out_shape=(jax.Sha...]
    mul x0 -> x1, other arithmetic: none -> 1.69 us  [on_device(): return (state_sum * mask_half, grad_sum * mask_half)]
    convert_element_type x0 -> x1, other arithmetic: none -> 0.72 us  [on_device(): mask_half = land_mask.astype(BF16)[None]]
where the time goes in v4:
time: 56.7 us; the launch traced here: 56 us
  Pallas kernels  53 us (93%)
  other arithmetic  2.41 us (4%)
  between operations  0.64 us (1%)
    pallas_call x1, Pallas kernels, on_device(): pl.pallas_call(functools.partial(block_kernel, sizes), out_shape=(jax.Sha...  53 us
    mul x1, other arithmetic, on_device(): return (state_sum * mask_half, grad_sum * mask_half)  1.69 us

profile of v4, /device:TPU:7, one launch (start us, length us, event | category | flops | bytes accessed | tf_op | source)
XLA Modules:
  0.0 56.0 jit_solution(1062030275393806344)
XLA Ops:
  0.6 0.7 %convert_element_type.3 = bf16[16,256]{1,0:T(8,128)(2,1)S(1)} convert(s32[16,256]{1,0:T(8,128)} %mask_hbm.1) | non-fusion elementwise | flops 4096 | bytes 24576 | tf_op jit(solution)/shard_map/convert_element_type | solution.py:599
  1.4 53.0 %ocean_block.1 = (bf16[16,16,256]{2,1,0:T(8,128)(2,1)}, bf16[16,16,256]{2,1,0:T(8,128)(2,1)}) custom-call(s32[3072]{0:T(1024)} %partner_hbm.1, bf16[16,16,256]{2,1,0:T(8,128)(2,1)} %state_hbm.1, s32[16,256]{1,0:T(8,128)} %mask_hbm.1, bf16[16,49]{1,0:T(8,128)(2,1)} %kernel_hbm.1, bf16[64,256]{1,0:T(8,128)(2,1)} %bitcast.1, bf16[64,256]{1,0:T(8,128)(2,1)} %project_hbm.1, ...), custom_call_target="tpu_custom_call" | custom-call | tf_op jit(solution)/shard_map/ocean_block/pallas_call | solution.py:554
  54.3 1.7 %broadcast_multiply_fusion = (bf16[16,16,256]{2,1,0:T(8,128)(2,1)}, bf16[16,16,256]{2,1,0:T(8,128)(2,1)}) fusion(bf16[16,16,256]{2,1,0:T(8,128)(2,1)} %get-tuple-element.5, bf16[16,256]{1,0:T(8,128)(2,1)S(1)} %convert_element_type.3, bf16[16,16,256]{2,1,0:T(8,128)(2,1)} %get-tuple-element.4), kind=kLoop, calls=%fused_computation | loop fusion | flops 131072 | bytes 532480 | tf_op jit(solution)/shard_map/mul | solution.py:600

commit v5 on v4

--- a/solution.py
+++ b/solution.py
@@ -54,6 +54,9 @@
     acc,
     edge_taps,
     edge_acc,
+    edge_out,
+    edge_in,
+    edge_tile,
     cot_rows,
     cot_all,
     depth_rows,
@@ -180,9 +183,25 @@
     loads[1].wait()
     mask_half = mask_ref[...].astype(BF16)
     masked = (state_ref[...] * mask_half[None]).reshape(cells, cols)
-    ext[own_rows, :, own_lanes] = (
-        dot(to_rows, masked).astype(BF16).reshape(rows, chans, cols)
-    )
+    own_cells = dot(to_rows, masked).astype(BF16)
+    ext[own_rows, :, own_lanes] = own_cells.reshape(rows, chans, cols)
+
+    slot = lax.broadcasted_iota(jnp.int32, (2 * 8, EDGE), 0)
+    spot = lax.broadcasted_iota(jnp.int32, (2 * 8, EDGE), 1)
+    first_cols = jnp.logical_and(slot < HALO, spot == slot).astype(BF16)
+    last_cols = jnp.logical_and(slot < HALO, spot == slot + EDGE - HALO).astype(BF16)
+
+    def pack_edges(block, phase):
+        edge_out[phase, 0] = dot(first_cols, block[:, :EDGE], ((1,), (1,))).astype(BF16)
+        edge_out[phase, 1] = dot(last_cols, block[:, cols - EDGE :], ((1,), (1,))).astype(BF16)
+
+    def unpack_edges(phase):
+        both = dot(edge_in[phase, 0], last_cols, ((0,), (0,))) + dot(
+            edge_in[phase, 1], first_cols, ((0,), (0,))
+        )
+        edge_tile[...] = both.reshape(rows, chans, EDGE)
+
+    pack_edges(own_cells, 0)
     @pl.when(lat == 0)
     def _():
         ext[0:HALO] = jnp.zeros((HALO, chans, wide), BF16)
@@ -201,9 +220,18 @@
 
     def halo_copy(buffer, d, send_sems, recv_sems):
         dl, do = DIRECTIONS[d]
+        if dl == 0:
+            phase = 0 if buffer is ext else 1
+            return pltpu.make_async_remote_copy(
+                src_ref=edge_out.at[phase, (1 + do) // 2],
+                dst_ref=edge_in.at[phase, (1 - do) // 2],
+                send_sem=send_sems.at[d],
+                recv_sem=recv_sems.at[d],
+                device_id=at(dl, do),
+                device_id_type=MESH,
+            )
         src_rows, dst_rows = {
             -1: (pl.ds(HALO, HALO), pl.ds(HALO + rows, HALO)),
-            0: (own_rows, own_rows),
             1: (pl.ds(rows, HALO), pl.ds(0, HALO)),
         }[dl]
         src_lanes, dst_lanes = {
@@ -281,11 +309,13 @@
         lax.fori_loop(0, n_ch, step, 0)
 
     def fold_start(buffer, gathered, k):
-        def step(i, carry):
+        def step(j, carry):
+            away = (j + 1) // 2
+            i = n_lon // 2 + away * (1 - 2 * lax.rem(j, 2))
             fold_copy(buffer, gathered, i, k).start()
             return carry
 
-        lax.fori_loop(1, n_lon, step, 0)
+        lax.fori_loop(0, n_lon - 1, step, 0)
 
     halo_start(ext, halo_send, halo_recv)
 
@@ -335,12 +365,11 @@
 
         lax.fori_loop(HALO, HALO + rows, step, 0, unroll=2)
 
-    def conv_edges(buffer, table):
+    def conv_edges(table):
         def step(e, carry):
-            left = jnp.where(lane >= EDGE // 2, buffer[e, :, pl.ds(0, EDGE)].astype(F32), 0.0)
-            right = jnp.where(
-                lane < EDGE // 2, buffer[e, :, pl.ds(EDGE + cols, EDGE)].astype(F32), 0.0
-            )
+            tile = edge_tile[e - HALO]
+            left = jnp.where(lane >= EDGE // 2, tile, 0.0)
+            right = jnp.where(lane < EDGE // 2, tile, 0.0)
             moved = [
                 jnp.where(
                     lane < EDGE // 2,
@@ -366,11 +395,7 @@
     def conv_total(start, count):
         edge = edge_acc[pl.ds(TAPS - 1 + start, count)]
         both = jnp.concatenate(
-            [
-                jnp.where(lane < EDGE // 2, edge, 0.0),
-                jnp.zeros((count, chans, cols - 2 * EDGE), F32),
-                jnp.where(lane < EDGE // 2, 0.0, edge),
-            ][:: 1 if cols > 2 * EDGE else 2],
+            [jnp.where(lane < EDGE // 2, edge, 0.0), jnp.where(lane < EDGE // 2, 0.0, edge)],
             axis=2,
         )
         return acc[pl.ds(TAPS - 1 + start, count)] + both
@@ -425,7 +450,8 @@
     for k in range(len(square)):
         square_copy(k).start()
     halo_arrived(ext, halo_send, halo_recv)
-    conv_edges(ext, 0)
+    unpack_edges(0)
+    conv_edges(0)
     conv_outer(ext, 0, below)
     depth_rows[pl.ds(0, settled)] = conv_total(0, settled).astype(BF16)
     channel_copies(
@@ -492,6 +518,7 @@
     channel_copies(lambda peer: mixed_send.at[peer], mixed_rows.at[me], 6)
 
     several(grad_send, n_ch, 5).wait_recv()
+    pack_edges(ext_back[own_rows, :, own_lanes].reshape(cells, cols), 1)
     halo_start(ext_back, halo_send_back, halo_recv_back)
 
     @pl.when(lat_last)
@@ -503,10 +530,13 @@
     to_chans = (swap_col == lax.rem(swap_row, rows) * chans + swap_row // rows).astype(BF16)
     several(mixed_rows, n_ch, 6).wait_recv()
     mixed_here = dot(to_chans, mixed_rows[...].reshape(cells, cols)).reshape(chans, rows, cols)
-    state_sum[...] = (state_ref[...].astype(F32) + mixed_here).astype(BF16)
+    state_sum[...] = (
+        mask_ref[...].astype(F32)[None] * (state_ref[...].astype(F32) + mixed_here)
+    ).astype(BF16)
 
     halo_arrived(ext_back, halo_send_back, halo_recv_back)
-    conv_edges(ext_back, 1)
+    unpack_edges(1)
+    conv_edges(1)
     conv_outer(ext_back, 1, below)
 
     @pl.when(lat_last)
@@ -541,11 +571,16 @@
     several(mixed_send, n_ch, 6).wait_send()
 
 
+def finish_kernel(state_sum, grad_sum, out_ref, grad_ref, sems):
+    out_ref[...] = state_sum[...]
+    grad_ref[...] = grad_sum[...]
+
+
 def on_device(state_field, land_mask, partner, kernel, w_expand, w_project, cotangent):
     n_lat, n_lon, n_ch = (lax.axis_size(name) for name in ("lat", "lon", "ch"))
     chans, rows, cols = state_field.shape
     hidden_here = w_project.shape[0]
-    assert rows == n_ch and n_lat % 2 == 0
+    assert rows == n_ch and n_lat == 4 and n_lon % 2 == 0 and cols == 2 * EDGE
     wide = cols + 2 * EDGE
     channels = n_ch * chans
     sizes = (n_lat, n_lon, n_ch, rows, chans, cols, hidden_here)
@@ -571,6 +606,9 @@
             pltpu.VMEM((rows + 2 * (TAPS - 1), chans, cols), F32),
             pltpu.VMEM((2, TAPS * HALO, chans, EDGE), F32),
             pltpu.VMEM((rows + 2 * (TAPS - 1), chans, EDGE), F32),
+            pltpu.VMEM((2, 2, 2 * 8, rows * chans), BF16),
+            pltpu.VMEM((2, 2, 2 * 8, rows * chans), BF16),
+            pltpu.VMEM((rows, chans, EDGE), F32),
             pltpu.VMEM((rows, chans, cols), BF16),
             pltpu.VMEM((n_ch, chans, cols), BF16),
             pltpu.VMEM((rows, chans, cols), BF16),
@@ -596,8 +634,15 @@
         ),
         name="ocean_block",
     )(partner, state_field, land_mask, kernel, w_expand.T, w_project, cotangent)
-    mask_half = land_mask.astype(BF16)[None]
-    return (state_sum * mask_half, grad_sum * mask_half)
+    anywhere = pl.BlockSpec(memory_space=pltpu.VMEM)
+    return pl.pallas_call(
+        finish_kernel,
+        out_shape=(jax.ShapeDtypeStruct(state_field.shape, BF16),) * 2,
+        in_specs=[anywhere] * 2,
+        out_specs=(anywhere, anywhere),
+        scratch_shapes=[pltpu.SemaphoreType.DMA((2,))],
+        name="finish",
+    )(state_sum, grad_sum)
 
 
 def solution(mesh):

time: 56.7 us -> 54.5 us (0.961)
  other arithmetic: 2.41 us -> 0 us
    pallas_call x0 -> x1, Pallas kernels: none -> 1.69 us  [on_device(): pl.pallas_call(finish_kernel, out_shape=(jax.ShapeDtypeStruct(state_field...]
    mul x1 -> x0, other arithmetic: 1.69 us -> none  [on_device(): return (state_sum * mask_half, grad_sum * mask_half)]
    pallas_call x1, Pallas kernels: 53 us -> 51.6 us  [on_device(): pl.pallas_call(functools.partial(block_kernel, sizes), out_shape=(jax.Sha...]
    convert_element_type x1 -> x0, other arithmetic: 0.72 us -> none  [on_device(): mask_half = land_mask.astype(BF16)[None]]
where the time goes in v5:
time: 54.5 us; the launch traced here: 53.9 us
  Pallas kernels  53.3 us (98%)
  between operations  0.64 us (1%)
    pallas_call x1, Pallas kernels, on_device(): pl.pallas_call(functools.partial(block_kernel, sizes), out_shape=(jax.Sha...  51.6 us
    pallas_call x1, Pallas kernels, on_device(): pl.pallas_call(finish_kernel, out_shape=(jax.ShapeDtypeStruct(state_field...  1.69 us

profile of v5, /device:TPU:7, one launch (start us, length us, event | category | flops | bytes accessed | tf_op | source)
XLA Modules:
  0.0 53.9 jit_solution(7536385162589838271)
XLA Ops:
  0.6 51.6 %ocean_block.1 = (bf16[16,16,256]{2,1,0:T(8,128)(2,1)}, bf16[16,16,256]{2,1,0:T(8,128)(2,1)}) custom-call(s32[3072]{0:T(1024)} %partner_hbm.1, bf16[16,16,256]{2,1,0:T(8,128)(2,1)} %state_hbm.1, s32[16,256]{1,0:T(8,128)} %mask_hbm.1, bf16[16,49]{1,0:T(8,128)(2,1)} %kernel_hbm.1, bf16[64,256]{1,0:T(8,128)(2,1)} %bitcast.1, bf16[64,256]{1,0:T(8,128)(2,1)} %project_hbm.1, ...), custom_call_target="tpu_custom_call" | custom-call | tf_op jit(solution)/shard_map/ocean_block/pallas_call | solution.py:589
  52.2 1.7 %finish.1 = (bf16[16,16,256]{2,1,0:T(8,128)(2,1)}, bf16[16,16,256]{2,1,0:T(8,128)(2,1)}) custom-call(bf16[16,16,256]{2,1,0:T(8,128)(2,1)} %get-tuple-element.4.state_sum, bf16[16,16,256]{2,1,0:T(8,128)(2,1)} %get-tuple-element.5.grad_sum), custom_call_target="tpu_custom_call" | custom-call | tf_op jit(solution)/shard_map/finish/pallas_call | solution.py:638

commit v6 on v5

--- a/solution.py
+++ b/solution.py
@@ -64,6 +64,7 @@
     weights,
     weights_send,
     normed_ref,
+    active_half,
     mixed_send,
     grad_send,
     mixed_rows,
@@ -494,16 +495,16 @@
     cot_here = cot_all[...].reshape(channels, cols)
     swap_weights(1 - part).wait_recv()
 
-    mixed = jnp.zeros((channels, cols), F32)
     back_norm = jnp.zeros((channels, cols), F32)
     per_chunk = n_ch // 4
-    for j in range(4):
-        span = slice(j * per_chunk, (j + 1) * per_chunk)
-        expand = weights[0, span].reshape(per_chunk * hidden_here, channels)
-        project = weights[1, span].reshape(per_chunk * hidden_here, channels)
+    chunk = per_chunk * hidden_here
+    chunks = [slice(j * per_chunk, (j + 1) * per_chunk) for j in range(4)]
+    for j, span in enumerate(chunks):
+        expand = weights[0, span].reshape(chunk, channels)
+        project = weights[1, span].reshape(chunk, channels)
         active, slope = gelu_parts(dot(expand, normed_half))
+        active_half[j] = active.astype(BF16)
         back_hidden = (dot(project, cot_here) * slope).astype(BF16)
-        mixed = mixed + dot(project, active.astype(BF16), ((0,), (0,)))
         back_norm = back_norm + dot(expand, back_hidden, ((0,), (0,)))
     normed = normed_ref[...]
     mean_plain = jnp.mean(back_norm, axis=0, keepdims=True)
@@ -514,8 +515,12 @@
         .reshape(n_ch, chans, cols)
     )
     channel_copies(lambda peer: grad_send.at[peer], ext_back.at[HALO + me, :, own_lanes], 5)
+    mixed = jnp.zeros((channels, cols), F32)
+    for j, span in enumerate(chunks):
+        mixed = mixed + dot(
+            weights[1, span].reshape(chunk, channels), active_half[j], ((0,), (0,))
+        )
     mixed_send[...] = mixed.astype(BF16).reshape(n_ch, chans, cols)
-    channel_copies(lambda peer: mixed_send.at[peer], mixed_rows.at[me], 6)
 
     several(grad_send, n_ch, 5).wait_recv()
     pack_edges(ext_back[own_rows, :, own_lanes].reshape(cells, cols), 1)
@@ -526,18 +531,18 @@
         fold_start(ext_back, fold_rows_back, 7)
         fold_rows_back[lon] = ext_back[pl.ds(rows, HALO), :, own_lanes]
 
+    channel_copies(lambda peer: mixed_send.at[peer], mixed_rows.at[me], 6)
     conv_own(ext_back, 1)
+    halo_arrived(ext_back, halo_send_back, halo_recv_back)
+    unpack_edges(1)
+    conv_edges(1)
+    conv_outer(ext_back, 1, below)
     to_chans = (swap_col == lax.rem(swap_row, rows) * chans + swap_row // rows).astype(BF16)
     several(mixed_rows, n_ch, 6).wait_recv()
     mixed_here = dot(to_chans, mixed_rows[...].reshape(cells, cols)).reshape(chans, rows, cols)
     state_sum[...] = (
         mask_ref[...].astype(F32)[None] * (state_ref[...].astype(F32) + mixed_here)
     ).astype(BF16)
-
-    halo_arrived(ext_back, halo_send_back, halo_recv_back)
-    unpack_edges(1)
-    conv_edges(1)
-    conv_outer(ext_back, 1, below)
 
     @pl.when(lat_last)
     def _():
@@ -616,6 +621,7 @@
             pltpu.VMEM((2, n_ch, hidden_here, channels), BF16),
             pltpu.VMEM((hidden_here // n_lat, channels), BF16),
             pltpu.VMEM((channels, cols), F32),
+            pltpu.VMEM((4, n_ch // 4 * hidden_here, cols), BF16),
             pltpu.VMEM((n_ch, chans, cols), BF16),
             pltpu.VMEM((n_ch, chans, cols), BF16),
             pltpu.VMEM((n_ch, chans, cols), BF16),

time: 54.5 us -> 53.7 us (0.985)
  the two profiles are of different devices: /device:TPU:7 before, /device:TPU:1 now
where the time goes in v6:
time: 53.7 us; the launch traced here: 53.5 us
  Pallas kernels  52.9 us (99%)
  between operations  0.64 us (1%)
    pallas_call x1, Pallas kernels, on_device(): pl.pallas_call(functools.partial(block_kernel, sizes), out_shape=(jax.Sha...  51.2 us
    pallas_call x1, Pallas kernels, on_device(): pl.pallas_call(finish_kernel, out_shape=(jax.ShapeDtypeStruct(state_field...  1.69 us

profile of v6, /device:TPU:1, one launch (start us, length us, event | category | flops | bytes accessed | tf_op | source)
XLA Modules:
  0.0 53.5 jit_solution(10235995368883008022)
XLA Ops:
  0.6 51.2 %ocean_block.1 = (bf16[16,16,256]{2,1,0:T(8,128)(2,1)}, bf16[16,16,256]{2,1,0:T(8,128)(2,1)}) custom-call(s32[3072]{0:T(1024)} %partner_hbm.1, bf16[16,16,256]{2,1,0:T(8,128)(2,1)} %state_hbm.1, s32[16,256]{1,0:T(8,128)} %mask_hbm.1, bf16[16,49]{1,0:T(8,128)(2,1)} %kernel_hbm.1, bf16[64,256]{1,0:T(8,128)(2,1)} %bitcast.1, bf16[64,256]{1,0:T(8,128)(2,1)} %project_hbm.1, ...), custom_call_target="tpu_custom_call" | custom-call | tf_op jit(solution)/shard_map/ocean_block/pallas_call | solution.py:594
  51.8 1.7 %finish.1 = (bf16[16,16,256]{2,1,0:T(8,128)(2,1)}, bf16[16,16,256]{2,1,0:T(8,128)(2,1)}) custom-call(bf16[16,16,256]{2,1,0:T(8,128)(2,1)} %get-tuple-element.4.state_sum, bf16[16,16,256]{2,1,0:T(8,128)(2,1)} %get-tuple-element.5.grad_sum), custom_call_target="tpu_custom_call" | custom-call | tf_op jit(solution)/shard_map/finish/pallas_call | solution.py:644

commit v7 on v6

--- a/solution.py
+++ b/solution.py
@@ -95,7 +95,7 @@
 
     mine, given = share_of(across), share_of(lat)
     lon_twin = lon + 1 - 2 * lax.rem(lon, 2)
-    square = [(0, 1)] + [(2 * i, j) for i in range(1, pairs) for j in (0, 1)]
+    square = [(2 * i, j) for i in range(1, pairs) for j in (1, 0)] + [(0, 1)]
 
     def in_square(turn, flip):
         return {
@@ -137,7 +137,7 @@
             pl.semaphore_signal(barrier, device_id=at(dl, do), device_id_type=MESH)
 
     lax.fori_loop(0, n_ch, greet_channel, 0)
-    for turn, flip in square[1:]:
+    for turn, flip in square[:-1]:
         if (turn, flip) == (pairs, 0):
             continue
         pl.semaphore_signal(barrier, device_id=in_square(turn, flip), device_id_type=MESH)

time: 53.7 us -> 53.3 us (level)
  the two profiles are of different devices: /device:TPU:1 before, /device:TPU:7 now
where the time goes in v7:
time: 53.3 us; the launch traced here: 52.9 us
  Pallas kernels  52.2 us (98%)
  between operations  0.64 us (1%)
    pallas_call x1, Pallas kernels, on_device(): pl.pallas_call(functools.partial(block_kernel, sizes), out_shape=(jax.Sha...  50.5 us
    pallas_call x1, Pallas kernels, on_device(): pl.pallas_call(finish_kernel, out_shape=(jax.ShapeDtypeStruct(state_field...  1.69 us

profile of v7, /device:TPU:7, one launch (start us, length us, event | category | flops | bytes accessed | tf_op | source)
XLA Modules:
  0.0 52.9 jit_solution(12076686420353978549)
XLA Ops:
  0.6 50.5 %ocean_block.1 = (bf16[16,16,256]{2,1,0:T(8,128)(2,1)}, bf16[16,16,256]{2,1,0:T(8,128)(2,1)}) custom-call(s32[3072]{0:T(1024)} %partner_hbm.1, bf16[16,16,256]{2,1,0:T(8,128)(2,1)} %state_hbm.1, s32[16,256]{1,0:T(8,128)} %mask_hbm.1, bf16[16,49]{1,0:T(8,128)(2,1)} %kernel_hbm.1, bf16[64,256]{1,0:T(8,128)(2,1)} %bitcast.1, bf16[64,256]{1,0:T(8,128)(2,1)} %project_hbm.1, ...), custom_call_target="tpu_custom_call" | custom-call | tf_op jit(solution)/shard_map/ocean_block/pallas_call | solution.py:594
  51.2 1.7 %finish.1 = (bf16[16,16,256]{2,1,0:T(8,128)(2,1)}, bf16[16,16,256]{2,1,0:T(8,128)(2,1)}) custom-call(bf16[16,16,256]{2,1,0:T(8,128)(2,1)} %get-tuple-element.4.state_sum, bf16[16,16,256]{2,1,0:T(8,128)(2,1)} %get-tuple-element.5.grad_sum), custom_call_target="tpu_custom_call" | custom-call | tf_op jit(solution)/shard_map/finish/pallas_call | solution.py:644
